TPU v7x, 256 devices: a whole 4x4x8 slice. The times are simulated.
256 devices in a mesh: gx: 8 (over x, core), gy: 32 (over z, y).
Axes of the slice: x: 4, y: 4, z: 8, core: 2. Of those that a mesh axis runs over, the one named last changes fastest.
Arguments:
- source: bfloat16 [16, 4096, 256], P(None, ('gx', 'gy')), may hold values from -6 to 6
- leaf_flux: bfloat16 [262144, 256], P(('gx', 'gy')), may hold values from -0.375 to 0.375
- leaf_particular: bfloat16 [1048576, 256], P(('gx', 'gy')), may hold values from -0.375 to 0.375
- leaf_lift: bfloat16 [262144, 256], P(('gx', 'gy')), may hold values from -0.75 to 0.75
- box_up: bfloat16 [163840, 1024], P(('gx', 'gy')), may hold values from -0.1875 to 0.1875
- box_down: bfloat16 [262144, 640], P(('gx', 'gy')), may hold values from -0.25 to 0.25
- up_one: bfloat16 [65536, 768], P(('gx', 'gy')), may hold values from -0.1875 to 0.1875
- down_one: bfloat16 [65536, 768], P(('gx', 'gy')), may hold values from -0.21875 to 0.21875
- up_two: bfloat16 [32768, 1536], P(('gx', 'gy')), may hold values from -0.125 to 0.125
- down_two: bfloat16 [32768, 1536], P(('gx', 'gy')), may hold values from -0.15625 to 0.15625
- up_root: bfloat16 [16384, 6144], P(('gx', 'gy')), may hold values from -0.046875 to 0.046875
- down_root: bfloat16 [16384, 6144], P(('gx', 'gy')), may hold values from -0.078125 to 0.078125
Outputs:
- solution: float32 [16, 4096, 256], P(None, ('gx', 'gy'))
All inputs are finite; a program needn't handle non-finite values.
Results may differ from a plain program's by a relative error of at most 0.014.
Values may be sent and summed in bfloat16 or wider, within the bound.
A program may use at most 64 MiB of HBM per device.

v0:
```python
import jax
import jax.numpy as jnp
from jax import lax
from jax.sharding import PartitionSpec as P


def partner(x, axis, stride):
    return lax.ppermute(x, axis, [(i, i ^ 1 << stride) for i in range(lax.axis_size(axis))])


def contract(left, right):
    return lax.dot_general(
        left, right, (((1,), (1,)), ((), ())), preferred_element_type=jnp.float32
    )


def place_pair(joined, other, place, bit_num):
    upper = place // 2**bit_num % 2 == 1
    lower = jnp.where(upper, other, joined)
    higher = jnp.where(upper, joined, other)
    return jnp.concatenate([lower, higher], axis=1)


def sum_sixteen(term):
    total = term
    for bit_num in range(4):
        total = total + partner(total.astype(jnp.bfloat16), ("gx", "gy"), bit_num).astype(
            total.dtype
        )
    return total


def join_sixteen(piece, place):
    joined = piece
    for bit_num in range(4):
        other = partner(joined, ("gx", "gy"), bit_num)
        joined = place_pair(joined, other, place, bit_num)
    return joined


def per_device(
    source,
    leaf_flux,
    leaf_particular,
    leaf_lift,
    box_up,
    box_down,
    up_one,
    down_one,
    up_two,
    down_two,
    up_root,
    down_root,
):
    rhs_count, leaves, points = source.shape
    edge_count = leaf_flux.shape[0] // leaves
    rows_count = lax.axis_size("gy")
    row_place = lax.axis_index("gy")
    place = lax.axis_index("gx") * rows_count + row_place
    k_zero = up_one.shape[0]
    inner_dev = box_up.shape[0] - k_zero
    second_width = up_two.shape[0]
    root_width = up_root.shape[0]
    flux = jnp.einsum(
        "rlq,leq->rle",
        source,
        leaf_flux.reshape(leaves, edge_count, points),
        preferred_element_type=jnp.float32,
    )
    flux = flux.astype(jnp.bfloat16).reshape(rhs_count, leaves * edge_count)
    box_state = contract(flux, box_up).astype(jnp.bfloat16)
    first_term = jnp.dot(box_state[:, inner_dev:], up_one, preferred_element_type=jnp.float32)
    first_sum = first_term
    for bit_num in range(2):
        first_sum = first_sum + partner(first_sum.astype(jnp.bfloat16), "gy", bit_num).astype(
            first_sum.dtype
        )
    first_state = first_sum.astype(jnp.bfloat16)
    k_one = first_state.shape[1] - k_zero
    second_piece = lax.dynamic_slice_in_dim(
        first_state, k_zero + place % 4 * second_width, second_width, 1
    )
    second_term = jnp.dot(second_piece, up_two, preferred_element_type=jnp.float32)
    second_sum = sum_sixteen(second_term)
    second_state = second_sum.astype(jnp.bfloat16)
    root_piece = lax.dynamic_slice_in_dim(
        second_state, k_one + place % 16 * root_width, root_width, 1
    )
    root_term = jnp.dot(root_piece, up_root, preferred_element_type=jnp.float32)
    root_state = lax.psum(root_term, ("gx", "gy")).astype(jnp.bfloat16)
    top_piece = contract(root_state, down_root).astype(jnp.bfloat16)
    top_bound = join_sixteen(top_piece, place)
    second_input = jnp.concatenate([second_state[:, :k_one], top_bound], axis=1)
    mid_piece = contract(second_input, down_two).astype(jnp.bfloat16)
    mid_bound = mid_piece
    for bit_num in range(2):
        other = partner(mid_bound, "gy", bit_num)
        mid_bound = place_pair(mid_bound, other, place, bit_num)
    first_input = jnp.concatenate([first_state[:, :k_zero], mid_bound], axis=1)
    box_bound = contract(first_input, down_one).astype(jnp.bfloat16)
    box_input = jnp.concatenate([box_state[:, :inner_dev], box_bound], axis=1)
    leaf_bound = (
        contract(box_input, box_down).astype(jnp.bfloat16).reshape(rhs_count, leaves, edge_count)
    )
    lifted = jnp.einsum(
        "rle,leq->rlq",
        leaf_bound,
        leaf_lift.reshape(leaves, edge_count, points),
        preferred_element_type=jnp.float32,
    )
    particular = jnp.einsum(
        "rlq,lqp->rlp",
        source,
        leaf_particular.reshape(leaves, points, points),
        preferred_element_type=jnp.float32,
    )
    return lifted + particular


def solution(mesh):
    return jax.shard_map(
        per_device,
        mesh=mesh,
        in_specs=(
            P(None, ("gx", "gy"), None),
            P(("gx", "gy"), None),
            P(("gx", "gy"), None),
            P(("gx", "gy"), None),
            P(("gx", "gy"), None),
            P(("gx", "gy"), None),
            P(("gx", "gy"), None),
            P(("gx", "gy"), None),
            P(("gx", "gy"), None),
            P(("gx", "gy"), None),
            P(("gx", "gy"), None),
            P(("gx", "gy"), None),
        ),
        out_specs=P(None, ("gx", "gy"), None),
        check_vma=False,
    )
```

profile of v0, /device:TPU:6, one launch (start us, length us, event | category | flops | bytes accessed | tf_op | source)
XLA Modules:
  0.0 143.0 jit_solution(12066938558323043604)
XLA Ops:
  0.0 1.4 %fusion.1 = bf16[16,16,64]{2,0,1:T(8,128)(2,1)S(1)} fusion(bf16[16,64,256]{2,1,0:T(8,128)(2,1)} %bitcast.25, bf16[16,16,256]{2,1,0:T(8,128)(2,1)} %param.12), kind=kOutput, calls=%fused_computation.4 | convolution fusion | flops 8404992 | bytes 688128 | tf_op jit(solution)/shard_map/rlq,leq->rle/dot_general | solution.py:64
  1.6 1.8 %convolution_convert_fusion.2 = bf16[16,640]{1,0:T(8,128)(2,1)S(1)} fusion(bf16[16,1024]{1,0:T(8,128)(2,1)S(1)} %reshape.16, bf16[640,1024]{1,0:T(8,128)(2,1)} %param.16), kind=kOutput, calls=%fused_computation.6 | convolution fusion | flops 20981760 | bytes 1363968 | tf_op jit(solution)/shard_map/dot_general | solution.py:12
  3.4 0.2 fusion.34
  3.6 1.6 %collective-permute-start = (bf16[16,768]{1,0:T(8,128)(2,1)S(1)}, bf16[16,768]{1,0:T(8,128)(2,1)S(1)}, u32[]{:S(2)}, u32[]{:S(2)}) collective-permute-start(bf16[16,768]{1,0:T(8,128)(2,1)S(1)} %get-tuple-element.17), channel_id=1, source_target_pairs={{0,1},{1,0},{2,3},{3,2},{4,5},{5,4},{6,7},{7,6},{8,9},{9,8},{10,11... | collective-permute-start | bytes 73736 | tf_op jit(solution)/shard_map/ppermute | solution.py:8
  5.3 2.2 %collective-permute-done = bf16[16,768]{1,0:T(8,128)(2,1)S(1)} collective-permute-done((bf16[16,768]{1,0:T(8,128)(2,1)S(1)}, bf16[16,768]{1,0:T(8,128)(2,1)S(1)}, u32[]{:S(2)}, u32[]{:S(2)}) %collective-permute-start) | collective-permute-done | bytes 24608 | tf_op jit(solution)/shard_map/ppermute | solution.py:8
  7.5 3.3 %collective-permute-start.1 = (bf16[16,768]{1,0:T(8,128)(2,1)S(1)}, bf16[16,768]{1,0:T(8,128)(2,1)S(1)}, u32[]{:S(2)}, u32[]{:S(2)}) collective-permute-start(bf16[16,768]{1,0:T(8,128)(2,1)S(1)} %fusion.13), channel_id=1, source_target_pairs={{0,2},{1,3},{2,0},{3,1},{4,6},{5,7},{6,4},{7,5},{8,10},{9,11},{10,... | collective-permute-start | bytes 73736 | tf_op jit(solution)/shard_map/ppermute | solution.py:8
  10.8 2.1 %collective-permute-done.1 = bf16[16,768]{1,0:T(8,128)(2,1)S(1)} collective-permute-done((bf16[16,768]{1,0:T(8,128)(2,1)S(1)}, bf16[16,768]{1,0:T(8,128)(2,1)S(1)}, u32[]{:S(2)}, u32[]{:S(2)}) %collective-permute-start.1) | collective-permute-done | bytes 24608 | tf_op jit(solution)/shard_map/ppermute | solution.py:8
  13.1 1.7 %collective-permute-start.2 = (bf16[16,1536]{1,0:T(8,128)(2,1)S(1)}, bf16[16,1536]{1,0:T(8,128)(2,1)S(1)}, u32[]{:S(2)}, u32[]{:S(2)}) collective-permute-start(bf16[16,1536]{1,0:T(8,128)(2,1)S(1)} %get-tuple-element.19), channel_id=1, source_target_pairs={{0,1},{1,0},{2,3},{3,2},{4,5},{5,4},{6,7},{7,6},{8,9},{9,8},{10,11... | collective-permute-start | bytes 147464 | tf_op jit(solution)/shard_map/ppermute | solution.py:8
  14.8 2.5 %collective-permute-done.2 = bf16[16,1536]{1,0:T(8,128)(2,1)S(1)} collective-permute-done((bf16[16,1536]{1,0:T(8,128)(2,1)S(1)}, bf16[16,1536]{1,0:T(8,128)(2,1)S(1)}, u32[]{:S(2)}, u32[]{:S(2)}) %collective-permute-start.2) | collective-permute-done | bytes 49184 | tf_op jit(solution)/shard_map/ppermute | solution.py:8
  17.3 3.7 %collective-permute-start.3 = (bf16[16,1536]{1,0:T(8,128)(2,1)S(1)}, bf16[16,1536]{1,0:T(8,128)(2,1)S(1)}, u32[]{:S(2)}, u32[]{:S(2)}) collective-permute-start(bf16[16,1536]{1,0:T(8,128)(2,1)S(1)} %fusion.5), channel_id=1, source_target_pairs={{0,2},{1,3},{2,0},{3,1},{4,6},{5,7},{6,4},{7,5},{8,10},{9,11},{10,... | collective-permute-start | bytes 147464 | tf_op jit(solution)/shard_map/ppermute | solution.py:8
  21.0 2.1 %collective-permute-done.3 = bf16[16,1536]{1,0:T(8,128)(2,1)S(1)} collective-permute-done((bf16[16,1536]{1,0:T(8,128)(2,1)S(1)}, bf16[16,1536]{1,0:T(8,128)(2,1)S(1)}, u32[]{:S(2)}, u32[]{:S(2)}) %collective-permute-start.3) | collective-permute-done | bytes 49184 | tf_op jit(solution)/shard_map/ppermute | solution.py:8
  23.1 2.0 %collective-permute-start.4 = (bf16[16,1536]{1,0:T(8,128)(2,1)S(1)}, bf16[16,1536]{1,0:T(8,128)(2,1)S(1)}, u32[]{:S(2)}, u32[]{:S(2)}) collective-permute-start(bf16[16,1536]{1,0:T(8,128)(2,1)S(1)} %fusion.33), channel_id=1, source_target_pairs={{0,4},{1,5},{2,6},{3,7},{4,0},{5,1},{6,2},{7,3},{8,12},{9,13},{10,... | collective-permute-start | bytes 147464 | tf_op jit(solution)/shard_map/ppermute | solution.py:8
  25.1 2.2 %collective-permute-done.4 = bf16[16,1536]{1,0:T(8,128)(2,1)S(1)} collective-permute-done((bf16[16,1536]{1,0:T(8,128)(2,1)S(1)}, bf16[16,1536]{1,0:T(8,128)(2,1)S(1)}, u32[]{:S(2)}, u32[]{:S(2)}) %collective-permute-start.4) | collective-permute-done | bytes 49184 | tf_op jit(solution)/shard_map/ppermute | solution.py:8
  27.3 3.4 %collective-permute-start.5 = (bf16[16,1536]{1,0:T(8,128)(2,1)S(1)}, bf16[16,1536]{1,0:T(8,128)(2,1)S(1)}, u32[]{:S(2)}, u32[]{:S(2)}) collective-permute-start(bf16[16,1536]{1,0:T(8,128)(2,1)S(1)} %fusion.6), channel_id=1, source_target_pairs={{0,8},{1,9},{2,10},{3,11},{4,12},{5,13},{6,14},{7,15},{8,0},{9,1},... | collective-permute-start | bytes 147464 | tf_op jit(solution)/shard_map/ppermute | solution.py:8
  30.7 2.1 %collective-permute-done.5 = bf16[16,1536]{1,0:T(8,128)(2,1)S(1)} collective-permute-done((bf16[16,1536]{1,0:T(8,128)(2,1)S(1)}, bf16[16,1536]{1,0:T(8,128)(2,1)S(1)}, u32[]{:S(2)}, u32[]{:S(2)}) %collective-permute-start.5) | collective-permute-done | bytes 49184 | tf_op jit(solution)/shard_map/ppermute | solution.py:8
  32.8 0.3 fusion.24
  33.1 80.1 %all-reduce.1 = bf16[16,6144]{1,0:T(8,128)(2,1)S(1)} all-reduce(f32[16,6144]{1,0:T(8,128)S(1)} %fusion.24), channel_id=1, replica_groups=mesh['gx'=8,'gy'=32] {'gx','gy'}, use_global_device_ids=true, to_apply=%region_0.1 | all-reduce | flops 98304 | bytes 589824 | tf_op jit(solution)/shard_map/psum | solution.py:90
  113.2 1.4 %convolution_convert_fusion.4 = bf16[16,64]{1,0:T(8,128)(2,1)S(1)} fusion(bf16[64,6144]{1,0:T(8,128)(2,1)} %param.23, bf16[16,6144]{1,0:T(8,128)(2,1)S(1)} %all-reduce.1), kind=kOutput, calls=%fused_computation.8 | convolution fusion | flops 12583936 | bytes 985088 | tf_op jit(solution)/shard_map/dot_general | solution.py:12
  114.7 3.6 %collective-permute-done.6 = bf16[16,64]{1,0:T(8,128)(2,1)S(1)} collective-permute-done((bf16[16,64]{1,0:T(8,128)(2,1)S(1)}, bf16[16,64]{1,0:T(8,128)(2,1)S(1)}, u32[]{:S(2)}, u32[]{:S(2)}) %collective-permute-start.6) | collective-permute-done | bytes 2080 | tf_op jit(solution)/shard_map/ppermute | solution.py:8
  118.4 0.9 collective-permute-start.7
  119.2 4.3 %collective-permute-done.7 = bf16[16,128]{1,0:T(8,128)(2,1)S(1)} collective-permute-done((bf16[16,128]{1,0:T(8,128)(2,1)S(1)}, bf16[16,128]{1,0:T(8,128)(2,1)S(1)}, u32[]{:S(2)}, u32[]{:S(2)}) %collective-permute-start.7) | collective-permute-done | bytes 4128 | tf_op jit(solution)/shard_map/ppermute | solution.py:8
  123.6 1.1 collective-permute-start.8
  124.7 2.6 %collective-permute-done.8 = bf16[16,256]{1,0:T(8,128)(2,1)S(1)} collective-permute-done((bf16[16,256]{1,0:T(8,128)(2,1)S(1)}, bf16[16,256]{1,0:T(8,128)(2,1)S(1)}, u32[]{:S(2)}, u32[]{:S(2)}) %collective-permute-start.8) | collective-permute-done | bytes 8224 | tf_op jit(solution)/shard_map/ppermute | solution.py:8
  127.3 0.5 collective-permute-start.9
  127.8 4.2 %collective-permute-done.9 = bf16[16,512]{1,0:T(8,128)(2,1)S(1)} collective-permute-done((bf16[16,512]{1,0:T(8,128)(2,1)S(1)}, bf16[16,512]{1,0:T(8,128)(2,1)S(1)}, u32[]{:S(2)}, u32[]{:S(2)}) %collective-permute-start.9) | collective-permute-done | bytes 16416 | tf_op jit(solution)/shard_map/ppermute | solution.py:8
  132.0 0.2 convolution_convert_fusion.5
  132.2 3.6 %collective-permute-done.10 = bf16[16,128]{1,0:T(8,128)(2,1)S(1)} collective-permute-done((bf16[16,128]{1,0:T(8,128)(2,1)S(1)}, bf16[16,128]{1,0:T(8,128)(2,1)S(1)}, u32[]{:S(2)}, u32[]{:S(2)}) %collective-permute-start.10) | collective-permute-done | bytes 4128 | tf_op jit(solution)/shard_map/ppermute | solution.py:8
  135.9 1.0 collective-permute-start.11
  136.8 0.4 convolution_bitcast_fusion.1
  137.2 3.9 %collective-permute-done.11 = bf16[16,256]{1,0:T(8,128)(2,1)S(1)} collective-permute-done((bf16[16,256]{1,0:T(8,128)(2,1)S(1)}, bf16[16,256]{1,0:T(8,128)(2,1)S(1)}, u32[]{:S(2)}, u32[]{:S(2)}) %collective-permute-start.11) | collective-permute-done | bytes 8224 | tf_op jit(solution)/shard_map/ppermute | solution.py:8
  141.3 0.5 convolution_convert_fusion.1
  142.1 0.9 copy.21
  (45 shorter events, 1.2 us)
Async XLA Ops:
  0.0 136.8 %copy-start = (bf16[4096,256]{1,0:T(8,128)(2,1)S(1)}, bf16[4096,256]{1,0:T(8,128)(2,1)}, u32[]{:S(2)}) copy-start(bf16[4096,256]{1,0:T(8,128)(2,1)} %param.14) | copy-start | bytes 6291460
  1.4 11.5 %copy-start.5 = (bf16[128,1536]{1,0:T(8,128)(2,1)S(1)}, bf16[128,1536]{1,0:T(8,128)(2,1)}, u32[]{:S(2)}) copy-start(bf16[128,1536]{1,0:T(8,128)(2,1)} %param.20) | copy-start | bytes 1179652
  1.6 1.8 %copy-start.8 = (bf16[256,768]{1,0:T(8,128)(2,1)S(1)}, bf16[256,768]{1,0:T(8,128)(2,1)}, u32[]{:S(2)}) copy-start(bf16[256,768]{1,0:T(8,128)(2,1)} %param.18) | copy-start | bytes 1179652
  3.4 29.4 %copy-start.2 = (bf16[64,6144]{1,0:T(8,128)(2,1)S(1)}, bf16[64,6144]{1,0:T(8,128)(2,1)}, u32[]{:S(2)}) copy-start(bf16[64,6144]{1,0:T(8,128)(2,1)} %param.22) | copy-start | bytes 2359300
  3.6 3.9 %collective-permute-start = (bf16[16,768]{1,0:T(8,128)(2,1)S(1)}, bf16[16,768]{1,0:T(8,128)(2,1)S(1)}, u32[]{:S(2)}, u32[]{:S(2)}) collective-permute-start(bf16[16,768]{1,0:T(8,128)(2,1)S(1)} %get-tuple-element.17), channel_id=1, source_target_pairs={{0,1},{1,0},{2,3},{3,2},{4,5},{5,4},{6,7},{7,6},{8,9},{9,8},{10,11... | collective-permute-start | bytes 73736 | tf_op jit(solution)/shard_map/ppermute | solution.py:8
  7.5 5.4 %collective-permute-start.1 = (bf16[16,768]{1,0:T(8,128)(2,1)S(1)}, bf16[16,768]{1,0:T(8,128)(2,1)S(1)}, u32[]{:S(2)}, u32[]{:S(2)}) collective-permute-start(bf16[16,768]{1,0:T(8,128)(2,1)S(1)} %fusion.13), channel_id=1, source_target_pairs={{0,2},{1,3},{2,0},{3,1},{4,6},{5,7},{6,4},{7,5},{8,10},{9,11},{10,... | collective-permute-start | bytes 73736 | tf_op jit(solution)/shard_map/ppermute | solution.py:8
  13.1 4.2 %collective-permute-start.2 = (bf16[16,1536]{1,0:T(8,128)(2,1)S(1)}, bf16[16,1536]{1,0:T(8,128)(2,1)S(1)}, u32[]{:S(2)}, u32[]{:S(2)}) collective-permute-start(bf16[16,1536]{1,0:T(8,128)(2,1)S(1)} %get-tuple-element.19), channel_id=1, source_target_pairs={{0,1},{1,0},{2,3},{3,2},{4,5},{5,4},{6,7},{7,6},{8,9},{9,8},{10,11... | collective-permute-start | bytes 147464 | tf_op jit(solution)/shard_map/ppermute | solution.py:8
  17.3 5.8 %collective-permute-start.3 = (bf16[16,1536]{1,0:T(8,128)(2,1)S(1)}, bf16[16,1536]{1,0:T(8,128)(2,1)S(1)}, u32[]{:S(2)}, u32[]{:S(2)}) collective-permute-start(bf16[16,1536]{1,0:T(8,128)(2,1)S(1)} %fusion.5), channel_id=1, source_target_pairs={{0,2},{1,3},{2,0},{3,1},{4,6},{5,7},{6,4},{7,5},{8,10},{9,11},{10,... | collective-permute-start | bytes 147464 | tf_op jit(solution)/shard_map/ppermute | solution.py:8
  23.1 4.2 %collective-permute-start.4 = (bf16[16,1536]{1,0:T(8,128)(2,1)S(1)}, bf16[16,1536]{1,0:T(8,128)(2,1)S(1)}, u32[]{:S(2)}, u32[]{:S(2)}) collective-permute-start(bf16[16,1536]{1,0:T(8,128)(2,1)S(1)} %fusion.33), channel_id=1, source_target_pairs={{0,4},{1,5},{2,6},{3,7},{4,0},{5,1},{6,2},{7,3},{8,12},{9,13},{10,... | collective-permute-start | bytes 147464 | tf_op jit(solution)/shard_map/ppermute | solution.py:8
  27.3 5.4 %collective-permute-start.5 = (bf16[16,1536]{1,0:T(8,128)(2,1)S(1)}, bf16[16,1536]{1,0:T(8,128)(2,1)S(1)}, u32[]{:S(2)}, u32[]{:S(2)}) collective-permute-start(bf16[16,1536]{1,0:T(8,128)(2,1)S(1)} %fusion.6), channel_id=1, source_target_pairs={{0,8},{1,9},{2,10},{3,11},{4,12},{5,13},{6,14},{7,15},{8,0},{9,1},... | collective-permute-start | bytes 147464 | tf_op jit(solution)/shard_map/ppermute | solution.py:8
  33.1 98.9 %copy-start.6 = (bf16[128,1536]{1,0:T(8,128)(2,1)S(1)}, bf16[128,1536]{1,0:T(8,128)(2,1)}, u32[]{:S(2)}) copy-start(bf16[128,1536]{1,0:T(8,128)(2,1)} %param.21) | copy-start | bytes 1179652
  33.1 103.7 %copy-start.4 = (bf16[16,16,256]{2,1,0:T(8,128)(2,1)S(1)}, bf16[16,16,256]{2,1,0:T(8,128)(2,1)}, u32[]{:S(2)}) copy-start(bf16[16,16,256]{2,1,0:T(8,128)(2,1)} %param.12) | copy-start | bytes 393220
  114.6 3.6 %collective-permute-start.6 = (bf16[16,64]{1,0:T(8,128)(2,1)S(1)}, bf16[16,64]{1,0:T(8,128)(2,1)S(1)}, u32[]{:S(2)}, u32[]{:S(2)}) collective-permute-start(bf16[16,64]{1,0:T(8,128)(2,1)S(1)} %convolution_convert_fusion.4), channel_id=1, source_target_pairs={{0,1},{1,0},{2,3},{3,2},{4,5},{5,4},{6,7},{7,6},{8,9},{9,8},{10,11... | collective-permute-start | bytes 6152 | tf_op jit(solution)/shard_map/ppermute | solution.py:8
  118.4 5.1 %collective-permute-start.7 = (bf16[16,128]{1,0:T(8,128)(2,1)S(1)}, bf16[16,128]{1,0:T(8,128)(2,1)S(1)}, u32[]{:S(2)}, u32[]{:S(2)}) collective-permute-start(bf16[16,128]{1,0:T(8,128)(2,1)S(1)} %pad_maximum_fusion.3), channel_id=1, source_target_pairs={{0,2},{1,3},{2,0},{3,1},{4,6},{5,7},{6,4},{7,5},{8,10},{9,11},{10,... | collective-permute-start | bytes 12296 | tf_op jit(solution)/shard_map/ppermute | solution.py:8
  123.6 3.7 %collective-permute-start.8 = (bf16[16,256]{1,0:T(8,128)(2,1)S(1)}, bf16[16,256]{1,0:T(8,128)(2,1)S(1)}, u32[]{:S(2)}, u32[]{:S(2)}) collective-permute-start(bf16[16,256]{1,0:T(8,128)(2,1)S(1)} %pad_maximum_fusion.1), channel_id=1, source_target_pairs={{0,4},{1,5},{2,6},{3,7},{4,0},{5,1},{6,2},{7,3},{8,12},{9,13},{10,... | collective-permute-start | bytes 24584 | tf_op jit(solution)/shard_map/ppermute | solution.py:8
  127.3 4.7 %collective-permute-start.9 = (bf16[16,512]{1,0:T(8,128)(2,1)S(1)}, bf16[16,512]{1,0:T(8,128)(2,1)S(1)}, u32[]{:S(2)}, u32[]{:S(2)}) collective-permute-start(bf16[16,512]{1,0:T(8,128)(2,1)S(1)} %pad_maximum_fusion), channel_id=1, source_target_pairs={{0,8},{1,9},{2,10},{3,11},{4,12},{5,13},{6,14},{7,15},{8,0},{9,1},... | collective-permute-start | bytes 49160 | tf_op jit(solution)/shard_map/ppermute | solution.py:8
  132.2 8.9 %copy-start.7 = (bf16[256,768]{1,0:T(8,128)(2,1)S(1)}, bf16[256,768]{1,0:T(8,128)(2,1)}, u32[]{:S(2)}) copy-start(bf16[256,768]{1,0:T(8,128)(2,1)} %param.19) | copy-start | bytes 1179652
  132.2 3.6 %collective-permute-start.10 = (bf16[16,128]{1,0:T(8,128)(2,1)S(1)}, bf16[16,128]{1,0:T(8,128)(2,1)S(1)}, u32[]{:S(2)}, u32[]{:S(2)}) collective-permute-start(bf16[16,128]{1,0:T(8,128)(2,1)S(1)} %convolution_convert_fusion.5), channel_id=1, source_target_pairs={{0,1},{1,0},{2,3},{3,2},{4,5},{5,4},{6,7},{7,6},{8,9},{9,8},{10,11... | collective-permute-start | bytes 12296 | tf_op jit(solution)/shard_map/ppermute | solution.py:8
  135.9 5.2 %collective-permute-start.11 = (bf16[16,256]{1,0:T(8,128)(2,1)S(1)}, bf16[16,256]{1,0:T(8,128)(2,1)S(1)}, u32[]{:S(2)}, u32[]{:S(2)}) collective-permute-start(bf16[16,256]{1,0:T(8,128)(2,1)S(1)} %pad_maximum_fusion.2), channel_id=1, source_target_pairs={{0,2},{1,3},{2,0},{3,1},{4,6},{5,7},{6,4},{7,5},{8,10},{9,11},{10,... | collective-permute-start | bytes 24584 | tf_op jit(solution)/shard_map/ppermute | solution.py:8
  136.8 4.5 %copy-start.1 = (bf16[1024,640]{1,0:T(8,128)(2,1)S(1)}, bf16[1024,640]{1,0:T(8,128)(2,1)}, u32[]{:S(2)}) copy-start(bf16[1024,640]{1,0:T(8,128)(2,1)} %param.17) | copy-start | bytes 3932164
  137.2 4.7 %copy-start.3 = (bf16[1024,256]{1,0:T(8,128)(2,1)S(1)}, bf16[1024,256]{1,0:T(8,128)(2,1)}, u32[]{:S(2)}) copy-start(bf16[1024,256]{1,0:T(8,128)(2,1)} %param.15) | copy-start | bytes 1572868
where the time goes:
time: 143 us
  blocking collectives  80.1 us (56%)
  waiting for transfers between devices  35.3 us (25%)
  starting transfers between devices  19.1 us (13%)
  matrix products  6.77 us (5%)
    psum x1, blocking collectives, per_device(): root_state = lax.psum(root_term, ('gx', 'gy')).astype(jnp.bfloat16)  80.1 us
    ppermute x12, waiting for transfers between devices, partner(): lax.ppermute(x, axis, [(i, i ^ 1 << stride) for i in range(lax.axis_size(...  35.3 us
    ppermute x12, starting transfers between devices, partner(): lax.ppermute(x, axis, [(i, i ^ 1 << stride) for i in range(lax.axis_size(...  19.1 us
    dot_general x5, matrix products, contract(): lax.dot_general(left, right, (((1,), (1,)), ((), ())), preferred_element_...  4.13 us
  transfers between devices with their start and end apart: 12, of which 12 were waited for; matrix products, arithmetic and copies ran while one was open for 0% of the time, Pallas kernels for 0%

commit v1 on v0

v1 whole, which is shorter than its diff:
```python
import jax
import jax.numpy as jnp
from jax import lax
from jax.experimental import pallas as pl
from jax.experimental.pallas import tpu as pltpu
from jax.sharding import PartitionSpec as P

MESH = pl.DeviceIdType.MESH
BF = jnp.bfloat16
F32 = jnp.float32

R = 16
LEAF = 16
ST_A, ST_AI, ST_B, ST_BI, ST_B2, ST_C1, ST_C2, ST_C3, ST_D, ST_E = range(10)
N_STAGE = 10


def nt(x, w):
    return lax.dot_general(x, w, (((1,), (1,)), ((), ())), preferred_element_type=F32)


def nn(x, w):
    return jnp.dot(x, w, preferred_element_type=F32)


def kernel(
    src_h, lf_h, lp_h, ll_h, bu_h, bd_h, u1_h, d1_h, u2_h, d2_h, ur_h, dr_h,
    out_ref,
    src, lf, lp, ll, bu, bd, u1, d1, u2, d2, ur, dr,
    sp, part, pre_leaf, pre_box, pre_mid,
    a_s, a_r, ai_s, ai_r,
    b_s, b_r, bi_r, si, b2_r,
    c1_s, c1_r, c2_s, c2_r, rs,
    d_s, d_r, d_all, e_s, e_r, e_all,
    load_sem, send_sem, recv_sem,
):
    gx = lax.axis_index("gx")
    gy = lax.axis_index("gy")
    x, core = gx // 2, gx % 2
    y, z = gy % 4, gy // 4
    zl, zh = z % 4, z // 4

    pairs = (
        (src_h, src), (lf_h, lf), (bu_h, bu), (u1_h, u1), (u2_h, u2), (lp_h, lp),
        (ur_h, ur), (bd_h, bd), (d1_h, d1), (d2_h, d2), (dr_h, dr), (ll_h, ll),
    )
    loads = [
        pltpu.make_async_copy(h, v, load_sem.at[i]) for i, (h, v) in enumerate(pairs)
    ]
    (l_src, l_lf, l_bu, l_u1, l_u2, l_lp, l_ur, l_bd, l_d1, l_d2, l_dr, l_ll) = loads
    for l in loads[:4]:
        l.start()

    def across(dx, dc, dy):
        return (((x + dx) % 4) * 2 + (core + dc) % 2, z * 4 + (y + dy) % 4)

    def in_plane(dz, dy):
        return (gx, (zh * 4 + (zl + dz) % 4) * 4 + (y + dy) % 4)

    def along_z(dz):
        return (gx, ((z + dz) % 8) * 4 + y)

    barrier = pltpu.get_barrier_semaphore()
    greet = []
    for dz in range(4):
        for dy in range(4):
            if dz or dy:
                greet.append(in_plane(dz, dy))
    for dx in range(4):
        for dc in range(2):
            for dy in range(4):
                if dx or dc:
                    greet.append(across(dx, dc, dy))
    for far in range(4):
        greet.append((gx, ((1 - zh) * 4 + far) * 4 + y))
    for device in greet:
        pl.semaphore_signal(barrier, inc=1, device_id=device, device_id_type=MESH)
    for l in loads[4:]:
        l.start()

    sends = []

    def send(s, d, stage, device):
        c = pltpu.make_async_remote_copy(
            src_ref=s,
            dst_ref=d,
            send_sem=send_sem.at[stage],
            recv_sem=recv_sem.at[stage],
            device_id=device,
            device_id_type=MESH,
        )
        c.start()

    def arrived(ref, stage):
        pltpu.make_async_copy(ref, ref, recv_sem.at[stage]).wait()

    def sent(ref, stage):
        pltpu.make_async_copy(ref, ref, send_sem.at[stage]).wait()

    l_src.wait()
    rows = lax.broadcasted_iota(jnp.int32, (256, 256), 0)
    cols = lax.broadcasted_iota(jnp.int32, (256, 256), 1)
    pick = ((rows % 16) * 16 + rows // 16 == cols).astype(F32).astype(BF)
    sp[...] = nn(pick, src[...].reshape(R * LEAF, 256)).astype(BF)
    l_lf.wait()
    lane = lax.broadcasted_iota(jnp.int32, (R, 128), 1)
    blocks = []
    for m in range(8):
        f = nt(sp[32 * m : 32 * m + 32, :], lf[128 * m : 128 * m + 128, :])
        blocks.append(jnp.where(lane < 64, f[:16], f[16:]).astype(BF))
    flux = jnp.concatenate(blocks, axis=1)
    l_bu.wait()
    box_flux = nt(flux, bu[384:, :]).astype(BF)
    l_u1.wait()
    first_flux = nn(box_flux, u1[:, 256:])
    for j in range(4):
        a_s[j] = first_flux[:, 128 * j : 128 * j + 128].astype(BF)
    pl.semaphore_wait(barrier, len(greet))
    for k in (2, 1, 3):
        send(a_s.at[(y + k) % 4], a_r.at[k - 1], ST_A, in_plane(0, k))
    first_if = nn(box_flux, u1[:, :256])
    ai_s[...] = first_if.astype(BF)
    for k in (2, 1, 3):
        send(ai_s, ai_r.at[k - 1], ST_AI, in_plane(0, k))
    box_if = nt(flux, bu[:384, :]).astype(BF)
    l_bd.wait()
    pre_leaf[...] = nt(box_if, bd[:, :384])
    l_u2.wait()

    arrived(a_r, ST_A)
    piece = a_s[y].astype(F32)
    for k in range(3):
        piece = piece + a_r[k].astype(F32)
    second_piece = piece.astype(BF)
    second_flux = nn(second_piece, u2[:, 512:])
    for j in range(8):
        b_s[4 + j] = second_flux[:, 128 * j : 128 * j + 128].astype(BF)
    plane = [(dz, dy) for dz in (2, 3, 1, 0) for dy in (2, 1, 3, 0) if dz or dy]
    for dz, dy in plane:
        to_z, to_y = (zl + dz) % 4, (y + dy) % 4
        send(
            b_s.at[4 + to_z * 2 + to_y // 2],
            b_r.at[dz * 4 + dy - 1],
            ST_B,
            in_plane(dz, dy),
        )
    second_if = nn(second_piece, u2[:, :512])
    for j in range(4):
        b_s[j] = second_if[:, 128 * j : 128 * j + 128].astype(BF)
    for dz, dy in plane:
        send(b_s.at[(zl + dz) % 4], bi_r.at[dz * 4 + dy - 1], ST_BI, in_plane(dz, dy))

    arrived(ai_r, ST_AI)
    whole = ai_s[...].astype(F32)
    for k in range(3):
        whole = whole + ai_r[k].astype(F32)
    l_d1.wait()
    pre_box[...] = nt(whole.astype(BF), d1[:, :256])
    l_lp.wait()
    for l in range(LEAF):
        part[l] = nn(sp[16 * l : 16 * l + 16, :], lp[256 * l : 256 * l + 256, :])
    l_ur.wait()

    arrived(b_r, ST_B)
    total = b_s[4 + zl * 2 + y // 2].astype(F32)
    for k in range(15):
        total = total + b_r[k].astype(F32)
    odd = jnp.broadcast_to(y % 2, (R, 64)) == 1
    root_piece = jnp.where(odd, total[:, 64:], total[:, :64]).astype(BF)
    for j in range(16):
        t = nn(root_piece, ur[:, 384 * j : 384 * j + 384])
        c1_s[0, j] = t[:8].astype(BF)
        c1_s[1, j] = t[8:].astype(BF)
    third = [
        (dx, dc, dy)
        for dx in (2, 1, 3, 0)
        for dy in (2, 1, 3, 0)
        for dc in (0, 1)
        if dx or dc or dy
    ]
    for dx, dc, dy in third:
        to = ((x + dx) % 4) * 4 + (y + dy) % 4
        send(
            c1_s.at[(core + dc) % 2, to],
            c1_r.at[(dx * 4 + dy) * 2 + dc - 1],
            ST_C1,
            across(dx, dc, dy),
        )
    arrived(bi_r, ST_BI)
    total = b_s[zl].astype(F32)
    for k in range(15):
        total = total + bi_r[k].astype(F32)
    si[zl] = total.astype(BF)
    for dz in (2, 1, 3):
        send(si.at[zl], si.at[zl], ST_B2, in_plane(dz, 0))
    l_d2.wait()
    l_dr.wait()
    l_ll.wait()

    arrived(c1_r, ST_C1)
    mine = c1_s[core, x * 4 + y].astype(F32)
    for k in range(31):
        mine = mine + c1_r[k].astype(F32)
    c2_s[...] = mine.astype(BF)
    for dz in (4, 3, 5, 2, 6, 1, 7):
        send(c2_s, c2_r.at[dz - 1], ST_C2, along_z(dz))
    arrived(b2_r, ST_B2)
    second_iface = jnp.concatenate([si[j] for j in range(4)], axis=1)
    pre_mid[...] = nt(second_iface, d2[:, :512])

    arrived(c2_r, ST_C2)
    for k in range(7):
        mine = mine + c2_r[k].astype(F32)
    rs[core, x * 4 + y] = mine.astype(BF)
    for dx, dc, dy in third:
        send(
            rs.at[core, x * 4 + y],
            rs.at[core, x * 4 + y],
            ST_C3,
            across(dx, dc, dy),
        )
    arrived(c1_r, ST_C3)
    top = jnp.zeros((R, 64), F32)
    for j in range(16):
        v = jnp.concatenate([rs[0, j].astype(F32), rs[1, j].astype(F32)], axis=0)
        top = top + nt(v.astype(BF), dr[:, 384 * j : 384 * j + 384])
    twice = jnp.concatenate([top, top], axis=1)
    half = jnp.broadcast_to(y % 2, (R, 128))
    here = zl * 4 + y
    d_all[here] = jnp.where(lane // 64 == half, twice, 0.0).astype(BF)
    for dz, dy in plane:
        send(d_all.at[here], d_all.at[here], ST_D, in_plane(dz, dy))
    arrived(b_r, ST_D)
    top_bound = jnp.concatenate(
        [d_all[2 * j] + d_all[2 * j + 1] for j in range(8)], axis=1
    )
    e_all[y] = (pre_mid[...] + nt(top_bound, d2[:, 512:])).astype(BF)
    for k in (2, 1, 3):
        send(e_all.at[y], e_all.at[y], ST_E, in_plane(0, k))
    arrived(a_r, ST_E)
    mid_bound = jnp.concatenate([e_all[j] for j in range(4)], axis=1)
    box_bound = (pre_box[...] + nt(mid_bound, d1[:, 256:])).astype(BF)
    leaf_bound = (pre_leaf[...] + nt(box_bound, bd[:, 384:])).astype(BF)
    low = lane < 64
    zero = jnp.zeros((R, 128), BF)
    for m in range(8):
        pair = leaf_bound[:, 128 * m : 128 * m + 128]
        both = jnp.concatenate(
            [jnp.where(low, pair, zero), jnp.where(low, zero, pair)], axis=0
        )
        lifted = nn(both, ll[128 * m : 128 * m + 128, :])
        out_ref[:, 2 * m, :] = lifted[:16] + part[2 * m]
        out_ref[:, 2 * m + 1, :] = lifted[16:] + part[2 * m + 1]

    sent(a_r, ST_A)
    sent(ai_r, ST_AI)
    sent(b_r, ST_B)
    sent(bi_r, ST_BI)
    sent(b2_r, ST_B2)
    sent(c1_r, ST_C1)
    sent(c2_r, ST_C2)
    sent(c1_r, ST_C3)
    sent(b_r, ST_D)
    sent(a_r, ST_E)


def per_device(*args):
    shapes = [a.shape for a in args]
    leaves = args[0].shape[1]
    return pl.pallas_call(
        kernel,
        out_shape=jax.ShapeDtypeStruct((R, leaves, 256), F32),
        in_specs=[pl.BlockSpec(memory_space=pl.ANY)] * 12,
        out_specs=pl.BlockSpec(memory_space=pltpu.VMEM),
        scratch_shapes=[pltpu.VMEM(s, BF) for s in shapes]
        + [
            pltpu.VMEM((256, 256), BF),
            pltpu.VMEM((16, 16, 256), F32),
            pltpu.VMEM((16, 1024), F32),
            pltpu.VMEM((16, 256), F32),
            pltpu.VMEM((16, 128), F32),
            pltpu.VMEM((4, 16, 128), BF),
            pltpu.VMEM((3, 16, 128), BF),
            pltpu.VMEM((16, 256), BF),
            pltpu.VMEM((3, 16, 256), BF),
            pltpu.VMEM((12, 16, 128), BF),
            pltpu.VMEM((15, 16, 128), BF),
            pltpu.VMEM((15, 16, 128), BF),
            pltpu.VMEM((4, 16, 128), BF),
            pltpu.VMEM((3, 16, 128), BF),
            pltpu.VMEM((2, 16, 8, 384), BF),
            pltpu.VMEM((31, 8, 384), BF),
            pltpu.VMEM((8, 384), BF),
            pltpu.VMEM((7, 8, 384), BF),
            pltpu.VMEM((2, 16, 8, 384), BF),
            pltpu.VMEM((16, 128), BF),
            pltpu.VMEM((15, 16, 128), BF),
            pltpu.VMEM((16, 16, 128), BF),
            pltpu.VMEM((16, 128), BF),
            pltpu.VMEM((3, 16, 128), BF),
            pltpu.VMEM((4, 16, 128), BF),
            pltpu.SemaphoreType.DMA((12,)),
            pltpu.SemaphoreType.DMA((N_STAGE,)),
            pltpu.SemaphoreType.DMA((N_STAGE,)),
        ],
        compiler_params=pltpu.CompilerParams(
            collective_id=0, has_side_effects=True, vmem_limit_bytes=60 * 1024 * 1024
        ),
    )(*args)


def solution(mesh):
    both = ("gx", "gy")
    return jax.shard_map(
        per_device,
        mesh=mesh,
        in_specs=(P(None, both, None),) + (P(both, None),) * 11,
        out_specs=P(None, both, None),
        check_vma=False,
    )
```

time: 143 us -> 45.6 us (0.32)
  the two profiles are of different devices: /device:TPU:6 before, /device:TPU:1 now
where the time goes in v1:
time: 45.6 us; the launch traced here: 45.5 us
  Pallas kernels  43.8 us (96%)
  local copies, waits for them, and re-layouts  1.67 us (4%)
    pallas_call x1, Pallas kernels, per_device(): pl.pallas_call(kernel, out_shape=jax.ShapeDtypeStruct((R, leaves, 256), F...  43.8 us
    unnamed x1, local copies, waits for them, and re-layouts  1.67 us

profile of v1, /device:TPU:1, one launch (start us, length us, event | category | flops | bytes accessed | tf_op | source)
XLA Modules:
  0.0 45.5 jit_solution(15814925780294430745)
XLA Ops:
  0.0 43.8 %shard_map.118 = f32[16,16,256]{2,1,0:T(8,128)} custom-call(bf16[16,16,256]{2,1,0:T(8,128)(2,1)} %src_h.1, bf16[1024,256]{1,0:T(8,128)(2,1)} %lf_h.1, bf16[4096,256]{1,0:T(8,128)(2,1)} %lp_h.1, bf16[1024,256]{1,0:T(8,128)(2,1)} %ll_h.1, bf16[640,1024]{1,0:T(8,128)(2,1)} %bu_h.1, bf16[1024,640]{1,0:T(8,128)(2,1)} %bd_h.1, bf16[256,768]{1,0:T(8,128)(2,1)} %u1_h.1, ...), custom_call_target="tpu_custom_call" | custom-call | tf_op jit(solution)/shard_map/pallas_call | solution.py:270
  43.8 1.7 %copy.14 = f32[16,16,256]{2,1,0:T(8,128)} copy(f32[16,16,256]{2,1,0:T(8,128)} %shard_map.118) | data formatting | bytes 524288

commit v2 on v1

v2 whole, which is shorter than its diff:
```python
import jax
import jax.numpy as jnp
from jax import lax
from jax.experimental import pallas as pl
from jax.experimental.pallas import tpu as pltpu
from jax.sharding import PartitionSpec as P

MESH = pl.DeviceIdType.MESH
BF = jnp.bfloat16
F32 = jnp.float32

R = 16
LEAF = 16
ST_A, ST_AI, ST_B, ST_BI, ST_B2, ST_C1, ST_C2, ST_C3, ST_D, ST_E = range(10)
N_STAGE = 10


def nt(x, w):
    return lax.dot_general(x, w, (((1,), (1,)), ((), ())), preferred_element_type=F32)


def nn(x, w):
    return jnp.dot(x, w, preferred_element_type=F32)


def kernel(
    src_h, lf_h, lp_h, bu_h, bd_h, u1_h, d1_h, u2_h, d2_h, ur_h, dr_h,
    lb_ref, part,
    src, lf, lp, bu, bd, u1, d1, u2, d2, ur, dr,
    sp, pre_leaf, pre_mid, joint,
    a_s, a_r, ai_s, ai_r,
    b_s, b_r, bi_s, bi_r, si, b2_r,
    c1_s, c1_r, c2_s, c2_r, rs,
    d_all, e_all,
    load_sem, send_sem, recv_sem,
):
    gx = lax.axis_index("gx")
    gy = lax.axis_index("gy")
    x, core = gx // 2, gx % 2
    y, z = gy % 4, gy // 4
    zl, zh = z % 4, z // 4

    pairs = (
        (src_h, src), (lf_h, lf), (bu_h.at[384:], bu.at[384:]), (u1_h, u1),
        (u2_h, u2), (ur_h, ur), (bu_h.at[:384], bu.at[:384]), (lp_h, lp),
        (bd_h, bd), (d1_h, d1), (d2_h, d2), (dr_h, dr),
    )
    loads = [
        pltpu.make_async_copy(h, v, load_sem.at[i]) for i, (h, v) in enumerate(pairs)
    ]
    (l_src, l_lf, l_bu, l_u1, l_u2, l_ur, l_bi, l_lp, l_bd, l_d1, l_d2, l_dr) = loads
    for l in loads[:4]:
        l.start()

    def across(dx, dc, dy):
        return (((x + dx) % 4) * 2 + (core + dc) % 2, z * 4 + (y + dy) % 4)

    def in_plane(dz, dy):
        return (gx, (zh * 4 + (zl + dz) % 4) * 4 + (y + dy) % 4)

    def along_z(dz):
        return (gx, ((z + dz) % 8) * 4 + y)

    barrier = pltpu.get_barrier_semaphore()
    greet = [(gx, ((1 - zh) * 4 + far) * 4 + y) for far in range(4)]
    plane = [(dz, dy) for dz in (2, 3, 1, 0) for dy in (2, 1, 3, 0) if dz or dy]
    third = [
        (dx, dc, dy)
        for dx in (2, 1, 3, 0)
        for dy in (2, 1, 3, 0)
        for dc in (0, 1)
        if dx or dc or dy
    ]
    greet += [in_plane(dz, dy) for dz, dy in plane]
    greet += [across(dx, dc, dy) for dx, dc, dy in third if dx or dc]
    for device in greet:
        pl.semaphore_signal(barrier, inc=1, device_id=device, device_id_type=MESH)

    def send(s, d, stage, device):
        c = pltpu.make_async_remote_copy(
            src_ref=s,
            dst_ref=d,
            send_sem=send_sem.at[stage],
            recv_sem=recv_sem.at[stage],
            device_id=device,
            device_id_type=MESH,
        )
        c.start()

    def arrived(ref, stage):
        pltpu.make_async_copy(ref, ref, recv_sem.at[stage]).wait()

    def sent(ref, stage):
        pltpu.make_async_copy(ref, ref, send_sem.at[stage]).wait()

    l_src.wait()
    rows = lax.broadcasted_iota(jnp.int32, (256, 256), 0)
    cols = lax.broadcasted_iota(jnp.int32, (256, 256), 1)
    pick = ((rows % 16) * 16 + rows // 16 == cols).astype(F32).astype(BF)
    sp[...] = nn(pick, src[...].reshape(R * LEAF, 256)).astype(BF)
    l_lf.wait()
    lane = lax.broadcasted_iota(jnp.int32, (R, 128), 1)
    low = lax.broadcasted_iota(jnp.int32, (8, 128), 1) < 64

    def pack(v):
        up, down = v[:8], v[8:]
        first = jnp.where(low, up, pltpu.roll(down, 64, 1))
        second = jnp.where(low, pltpu.roll(up, 64, 1), down)
        return first.astype(BF), second.astype(BF)

    def unpack(first, second):
        first, second = first.astype(F32), second.astype(F32)
        up = jnp.where(low, first, pltpu.roll(second, 64, 1))
        down = jnp.where(low, pltpu.roll(first, 64, 1), second)
        return jnp.concatenate([up, down], axis=0).astype(BF)

    blocks = []
    for m in range(8):
        f = nt(sp[32 * m : 32 * m + 32, :], lf[128 * m : 128 * m + 128, :])
        blocks.append(jnp.where(lane < 64, f[:16], f[16:]).astype(BF))
    flux = jnp.concatenate(blocks, axis=1)
    l_bu.wait()
    box_flux = nt(flux, bu[384:, :]).astype(BF)
    l_u1.wait()
    for l in loads[4:]:
        l.start()
    first_flux = nn(box_flux, u1[:, 256:])
    for j in range(4):
        a_s[j] = first_flux[:, 128 * j : 128 * j + 128].astype(BF)
    pl.semaphore_wait(barrier, len(greet))
    for k in (2, 1, 3):
        send(a_s.at[(y + k) % 4], a_r.at[k - 1], ST_A, in_plane(0, k))
    first_if = nn(box_flux, u1[:, :256])
    ai_s[...] = first_if.astype(BF)
    for k in (2, 1, 3):
        send(ai_s, ai_r.at[k - 1], ST_AI, in_plane(0, k))
    l_u2.wait()

    arrived(a_r, ST_A)
    piece = a_s[y].astype(F32)
    for k in range(3):
        piece = piece + a_r[k].astype(F32)
    second_piece = piece.astype(BF)
    second_flux = nn(second_piece, u2[:, 512:])
    for j in range(8):
        b_s[2 * j], b_s[2 * j + 1] = pack(second_flux[:, 128 * j : 128 * j + 128])
    for dz, dy in plane:
        to = (zl + dz) % 4 * 4 + (y + dy) % 4
        send(b_s.at[to], b_r.at[dz * 4 + dy - 1], ST_B, in_plane(dz, dy))
    second_if = nn(second_piece, u2[:, :512])
    for j in range(4):
        bi_s[2 * j], bi_s[2 * j + 1] = pack(second_if[:, 128 * j : 128 * j + 128])
    l_bi.wait()
    box_if = nt(flux, bu[:384, :]).astype(BF)
    l_ur.wait()

    arrived(b_r, ST_B)
    here = zl * 4 + y
    total = b_s[here].astype(F32)
    for k in range(15):
        total = total + b_r[k].astype(F32)
    root_piece = jnp.concatenate([total[:, :64], total[:, 64:]], axis=0).astype(BF)
    for j in range(16):
        t = nn(root_piece, ur[:, 384 * j : 384 * j + 384])
        c1_s[0, j] = t[:8].astype(BF)
        c1_s[1, j] = t[8:].astype(BF)
    for dx, dc, dy in third:
        to = ((x + dx) % 4) * 4 + (y + dy) % 4
        send(
            c1_s.at[(core + dc) % 2, to],
            c1_r.at[(dx * 4 + dy) * 2 + dc - 1],
            ST_C1,
            across(dx, dc, dy),
        )
    for dz, dy in plane:
        to = (zl + dz) % 2 * 4 + (y + dy) % 4
        send(bi_s.at[to], bi_r.at[dz * 4 + dy - 1], ST_BI, in_plane(dz, dy))
    l_lp.wait()
    for l in range(LEAF):
        part[l] = nn(sp[16 * l : 16 * l + 16, :], lp[256 * l : 256 * l + 256, :])
    arrived(ai_r, ST_AI)
    whole = ai_s[...].astype(F32)
    for k in range(3):
        whole = whole + ai_r[k].astype(F32)
    l_d1.wait()
    l_bd.wait()
    box_part = nt(whole.astype(BF), d1[:, :256]).astype(BF)
    pre_leaf[...] = nt(box_if, bd[:, :384]) + nt(box_part, bd[:, 384:])
    l_d2.wait()
    l_dr.wait()

    arrived(c1_r, ST_C1)
    mine = c1_s[core, x * 4 + y].astype(F32)
    for k in range(31):
        mine = mine + c1_r[k].astype(F32)
    c2_s[...] = mine.astype(BF)
    for dz in (4, 3, 5, 2, 6, 1, 7):
        send(c2_s, c2_r.at[dz - 1], ST_C2, along_z(dz))
    arrived(bi_r, ST_BI)
    own = zl % 2 * 4 + y
    total = bi_s[own].astype(F32)
    for k in range(15):
        total = total + bi_r[k].astype(F32)
    si[own] = total.astype(BF)
    flip = zl + 1 - zl % 2 * 2
    for dy in (2, 1, 3, 0):
        send(si.at[own], si.at[own], ST_B2, (gx, (zh * 4 + flip) * 4 + (y + dy) % 4))
    for dy in (2, 1, 3):
        send(si.at[own], si.at[own], ST_B2, in_plane(0, dy))

    arrived(c2_r, ST_C2)
    for k in range(7):
        mine = mine + c2_r[k].astype(F32)
    rs[core, x * 4 + y] = mine.astype(BF)
    for dx, dc, dy in third:
        send(
            rs.at[core, x * 4 + y],
            rs.at[core, x * 4 + y],
            ST_C3,
            across(dx, dc, dy),
        )
    for h in range(2):
        joint[:, 256 * h : 256 * h + 256] = nn(
            bd[:, 384:], d1[:, 256 + 256 * h : 512 + 256 * h]
        ).astype(BF)
    arrived(b2_r, ST_B2)
    second_iface = jnp.concatenate(
        [unpack(si[2 * j], si[2 * j + 1]) for j in range(4)], axis=1
    )
    pre_mid[...] = nt(second_iface, d2[:, :512])
    arrived(c1_r, ST_C3)
    top = jnp.zeros((R, 64), F32)
    for j in range(16):
        v = jnp.concatenate([rs[0, j].astype(F32), rs[1, j].astype(F32)], axis=0)
        top = top + nt(v.astype(BF), dr[:, 384 * j : 384 * j + 384])
    d_all[here] = jnp.concatenate([top[:8], top[8:]], axis=1).astype(BF)
    for dz, dy in plane:
        send(d_all.at[here], d_all.at[here], ST_D, in_plane(dz, dy))
    arrived(b_r, ST_D)
    top_bound = jnp.concatenate(
        [unpack(d_all[2 * j], d_all[2 * j + 1]) for j in range(8)], axis=1
    )
    e_all[y] = (pre_mid[...] + nt(top_bound, d2[:, 512:])).astype(BF)
    for k in (2, 1, 3):
        send(e_all.at[y], e_all.at[y], ST_E, in_plane(0, k))
    arrived(a_r, ST_E)
    mid_bound = jnp.concatenate([e_all[j] for j in range(4)], axis=1)
    lb_ref[...] = (pre_leaf[...] + nt(mid_bound, joint[...])).astype(BF)

    sent(a_r, ST_A)
    sent(ai_r, ST_AI)
    sent(b_r, ST_B)
    sent(bi_r, ST_BI)
    sent(b2_r, ST_B2)
    sent(c1_r, ST_C1)
    sent(c2_r, ST_C2)
    sent(c1_r, ST_C3)
    sent(b_r, ST_D)
    sent(a_r, ST_E)


def lift(lb_ref, part_ref, ll_ref, out_ref):
    low = lax.broadcasted_iota(jnp.int32, (R, 128), 1) < 64
    zero = jnp.zeros((R, 128), BF)
    for m in range(8):
        pair = lb_ref[:, 128 * m : 128 * m + 128]
        both = jnp.concatenate(
            [jnp.where(low, pair, zero), jnp.where(low, zero, pair)], axis=0
        )
        lifted = nn(both, ll_ref[128 * m : 128 * m + 128, :])
        out_ref[:, 2 * m, :] = lifted[:16] + part_ref[2 * m]
        out_ref[:, 2 * m + 1, :] = lifted[16:] + part_ref[2 * m + 1]


def per_device(src, lf, lp, ll, bu, bd, u1, d1, u2, d2, ur, dr):
    args = (src, lf, lp, bu, bd, u1, d1, u2, d2, ur, dr)
    vmem = pl.BlockSpec(memory_space=pltpu.VMEM)
    lb, part = pl.pallas_call(
        kernel,
        out_shape=(
            jax.ShapeDtypeStruct((R, 1024), BF),
            jax.ShapeDtypeStruct((LEAF, R, 256), F32),
        ),
        in_specs=[pl.BlockSpec(memory_space=pltpu.HBM)] * 11,
        out_specs=(vmem, vmem),
        scratch_shapes=[pltpu.VMEM(a.shape, BF) for a in args]
        + [
            pltpu.VMEM((256, 256), BF),
            pltpu.VMEM((16, 1024), F32),
            pltpu.VMEM((16, 128), F32),
            pltpu.VMEM((1024, 512), BF),
            pltpu.VMEM((4, 16, 128), BF),
            pltpu.VMEM((3, 16, 128), BF),
            pltpu.VMEM((16, 256), BF),
            pltpu.VMEM((3, 16, 256), BF),
            pltpu.VMEM((16, 8, 128), BF),
            pltpu.VMEM((15, 8, 128), BF),
            pltpu.VMEM((8, 8, 128), BF),
            pltpu.VMEM((15, 8, 128), BF),
            pltpu.VMEM((8, 8, 128), BF),
            pltpu.VMEM((7, 8, 128), BF),
            pltpu.VMEM((2, 16, 8, 384), BF),
            pltpu.VMEM((31, 8, 384), BF),
            pltpu.VMEM((8, 384), BF),
            pltpu.VMEM((7, 8, 384), BF),
            pltpu.VMEM((2, 16, 8, 384), BF),
            pltpu.VMEM((16, 8, 128), BF),
            pltpu.VMEM((4, 16, 128), BF),
            pltpu.SemaphoreType.DMA((12,)),
            pltpu.SemaphoreType.DMA((N_STAGE,)),
            pltpu.SemaphoreType.DMA((N_STAGE,)),
        ],
        compiler_params=pltpu.CompilerParams(
            collective_id=0, has_side_effects=True, vmem_limit_bytes=32 * 1024 * 1024
        ),
    )(*[pltpu.with_memory_space_constraint(a, pltpu.HBM) for a in args])
    return pl.pallas_call(
        lift,
        out_shape=jax.ShapeDtypeStruct((R, LEAF, 256), F32),
        in_specs=[vmem] * 3,
        out_specs=vmem,
        compiler_params=pltpu.CompilerParams(vmem_limit_bytes=8 * 1024 * 1024),
    )(lb, part, ll)


def solution(mesh):
    both = ("gx", "gy")
    return jax.shard_map(
        per_device,
        mesh=mesh,
        in_specs=(P(None, both, None),) + (P(both, None),) * 11,
        out_specs=P(None, both, None),
        check_vma=False,
    )
```

time: 45.6 us -> 43.7 us (0.958)
  local copies, waits for them, and re-layouts: 1.67 us -> 0.01 us
    unnamed x1 -> x2, local copies, waits for them, and re-layouts: 1.67 us -> 0.01 us
    pallas_call x1 -> x2, Pallas kernels: 43.8 us -> 43.6 us  [the longest x1 42.6 us: per_device(): pl.pallas_call(kernel, out_shape=(jax.ShapeDtypeStruct((R, 1024), BF), ja...]
where the time goes in v2:
time: 43.7 us; the launch traced here: 43.6 us
  Pallas kernels  43.6 us (100%)
    pallas_call x1, Pallas kernels, per_device(): pl.pallas_call(kernel, out_shape=(jax.ShapeDtypeStruct((R, 1024), BF), ja...  42.6 us
    pallas_call x1, Pallas kernels, per_device(): pl.pallas_call(lift, out_shape=jax.ShapeDtypeStruct((R, LEAF, 256), F32),...  0.94 us

profile of v2, /device:TPU:1, one launch (start us, length us, event | category | flops | bytes accessed | tf_op | source)
XLA Modules:
  0.0 43.6 jit_solution(13535519321444310382)
XLA Ops:
  0.0 0.0 copy-start
  0.0 42.6 %shard_map.118 = (bf16[16,1024]{1,0:T(8,128)(2,1)S(1)}, f32[16,16,256]{2,1,0:T(8,128)S(1)}) custom-call(bf16[16,16,256]{2,1,0:T(8,128)(2,1)} %src_h.1, bf16[1024,256]{1,0:T(8,128)(2,1)} %lf_h.1, bf16[4096,256]{1,0:T(8,128)(2,1)} %lp_h.1, bf16[640,1024]{1,0:T(8,128)(2,1)} %bu_h.1, bf16[1024,640]{1,0:T(8,128)(2,1)} %bd_h.1, bf16[256,768]{1,0:T(8,128)(2,1)} %u1_h.1, ...), custom_call_target="tpu_custom_call" | custom-call | tf_op jit(solution)/shard_map/pallas_call | solution.py:278
  42.6 0.0 copy-done
  42.6 0.9 %shard_map.119 = f32[16,16,256]{2,1,0:T(8,128)} custom-call(bf16[16,1024]{1,0:T(8,128)(2,1)S(1)} %get-tuple-element.7.lb_ref, f32[16,16,256]{2,1,0:T(8,128)S(1)} %get-tuple-element.8.part_ref, bf16[1024,256]{1,0:T(8,128)(2,1)S(1)} %copy-done), custom_call_target="tpu_custom_call" | custom-call | tf_op jit(solution)/shard_map/pallas_call | solution.py:317
Async XLA Ops:
  0.0 42.6 %copy-start = (bf16[1024,256]{1,0:T(8,128)(2,1)S(1)}, bf16[1024,256]{1,0:T(8,128)(2,1)}, u32[]{:S(2)}) copy-start(bf16[1024,256]{1,0:T(8,128)(2,1)} %ll_ref.1) | copy-start | bytes 1572868

commit v3 on v2

--- a/solution.py
+++ b/solution.py
@@ -11,8 +11,9 @@
 
 R = 16
 LEAF = 16
-ST_A, ST_AI, ST_B, ST_BI, ST_B2, ST_C1, ST_C2, ST_C3, ST_D, ST_E = range(10)
-N_STAGE = 10
+ST_A, ST_AI, ST_B, ST_BI, ST_B2, ST_C1, ST_C2, ST_D, ST_E = range(9)
+ST_X, ST_C3, ST_F = 9, 13, 17
+N_STAGE = 21
 
 
 def nt(x, w):
@@ -30,9 +31,9 @@
     sp, pre_leaf, pre_mid, joint,
     a_s, a_r, ai_s, ai_r,
     b_s, b_r, bi_s, bi_r, si, b2_r,
-    c1_s, c1_r, c2_s, c2_r, rs,
+    c1_s, c1_x, c1_t, c1_r, c2_s, c2_r, rs,
     d_all, e_all,
-    load_sem, send_sem, recv_sem,
+    load_sem, send_sem, recv_sem, round_sem,
 ):
     gx = lax.axis_index("gx")
     gy = lax.axis_index("gy")
@@ -52,8 +53,10 @@
     for l in loads[:4]:
         l.start()
 
-    def across(dx, dc, dy):
-        return (((x + dx) % 4) * 2 + (core + dc) % 2, z * 4 + (y + dy) % 4)
+    sibling = (x * 2 + 1 - core, gy)
+
+    def across(dx, dy):
+        return ((x + dx) % 4 * 2 + core, z * 4 + (y + dy) % 4)
 
     def in_plane(dz, dy):
         return (gx, (zh * 4 + (zl + dz) % 4) * 4 + (y + dy) % 4)
@@ -61,20 +64,26 @@
     def along_z(dz):
         return (gx, ((z + dz) % 8) * 4 + y)
 
+    x_near = [across(1, 0), across(3, 0)]
+    z_near = [along_z(1), along_z(7)]
+    greet = [in_plane(0, 2), in_plane(0, 1), in_plane(0, 3), sibling] + z_near + x_near
+    rounds = (z_near, z_near + x_near, z_near + x_near)
     barrier = pltpu.get_barrier_semaphore()
-    greet = [(gx, ((1 - zh) * 4 + far) * 4 + y) for far in range(4)]
-    plane = [(dz, dy) for dz in (2, 3, 1, 0) for dy in (2, 1, 3, 0) if dz or dy]
-    third = [
-        (dx, dc, dy)
-        for dx in (2, 1, 3, 0)
-        for dy in (2, 1, 3, 0)
-        for dc in (0, 1)
-        if dx or dc or dy
-    ]
-    greet += [in_plane(dz, dy) for dz, dy in plane]
-    greet += [across(dx, dc, dy) for dx, dc, dy in third if dx or dc]
     for device in greet:
         pl.semaphore_signal(barrier, inc=1, device_id=device, device_id_type=MESH)
+
+    def pass_on(n):
+        if n == 0:
+            pl.semaphore_wait(barrier, len(greet))
+        else:
+            pl.semaphore_wait(round_sem.at[n - 1], len(rounds[n - 1]))
+        if n < 3:
+            for device in rounds[n]:
+                pl.semaphore_signal(
+                    round_sem.at[n], inc=1, device_id=device, device_id_type=MESH
+                )
+
+    plane = [(dz, dy) for dz in (2, 3, 1, 0) for dy in (2, 1, 3, 0) if dz or dy]
 
     def send(s, d, stage, device):
         c = pltpu.make_async_remote_copy(
@@ -119,6 +128,7 @@
         f = nt(sp[32 * m : 32 * m + 32, :], lf[128 * m : 128 * m + 128, :])
         blocks.append(jnp.where(lane < 64, f[:16], f[16:]).astype(BF))
     flux = jnp.concatenate(blocks, axis=1)
+    pass_on(0)
     l_bu.wait()
     box_flux = nt(flux, bu[384:, :]).astype(BF)
     l_u1.wait()
@@ -127,13 +137,14 @@
     first_flux = nn(box_flux, u1[:, 256:])
     for j in range(4):
         a_s[j] = first_flux[:, 128 * j : 128 * j + 128].astype(BF)
-    pl.semaphore_wait(barrier, len(greet))
     for k in (2, 1, 3):
         send(a_s.at[(y + k) % 4], a_r.at[k - 1], ST_A, in_plane(0, k))
+    pass_on(1)
     first_if = nn(box_flux, u1[:, :256])
     ai_s[...] = first_if.astype(BF)
     for k in (2, 1, 3):
         send(ai_s, ai_r.at[k - 1], ST_AI, in_plane(0, k))
+    pass_on(2)
     l_u2.wait()
 
     arrived(a_r, ST_A)
@@ -144,6 +155,7 @@
     second_flux = nn(second_piece, u2[:, 512:])
     for j in range(8):
         b_s[2 * j], b_s[2 * j + 1] = pack(second_flux[:, 128 * j : 128 * j + 128])
+    pass_on(3)
     for dz, dy in plane:
         to = (zl + dz) % 4 * 4 + (y + dy) % 4
         send(b_s.at[to], b_r.at[dz * 4 + dy - 1], ST_B, in_plane(dz, dy))
@@ -160,18 +172,34 @@
     for k in range(15):
         total = total + b_r[k].astype(F32)
     root_piece = jnp.concatenate([total[:, :64], total[:, 64:]], axis=0).astype(BF)
-    for j in range(16):
-        t = nn(root_piece, ur[:, 384 * j : 384 * j + 384])
-        c1_s[0, j] = t[:8].astype(BF)
-        c1_s[1, j] = t[8:].astype(BF)
-    for dx, dc, dy in third:
-        to = ((x + dx) % 4) * 4 + (y + dy) % 4
+    reach = (2, 1, 3, 0)
+    for n, dx in enumerate(reach):
+        g = (x + dx) % 4
+        t = nn(root_piece, ur[:, pl.ds(pl.multiple_of(1536 * g, 128), 1536)])
+        for q in range(4):
+            c1_s[0, 4 * g + q] = t[:8, 384 * q : 384 * q + 384].astype(BF)
+            c1_s[1, 4 * g + q] = t[8:, 384 * q : 384 * q + 384].astype(BF)
         send(
-            c1_s.at[(core + dc) % 2, to],
-            c1_r.at[(dx * 4 + dy) * 2 + dc - 1],
-            ST_C1,
-            across(dx, dc, dy),
+            c1_s.at[1 - core, pl.ds(4 * g, 4)],
+            c1_x.at[pl.ds(4 * g, 4)],
+            ST_X + n,
+            sibling,
         )
+    for n, dx in enumerate(reach):
+        g = (x + dx) % 4
+        arrived(c1_r.at[:4], ST_X + n)
+        for q in range(4):
+            c1_t[4 * g + q] = (
+                c1_s[core, 4 * g + q].astype(F32) + c1_x[4 * g + q].astype(F32)
+            ).astype(BF)
+        for dy in (2, 1, 3, 0):
+            if dx or dy:
+                send(
+                    c1_t.at[4 * g + (y + dy) % 4],
+                    c1_r.at[dx * 4 + dy - 1],
+                    ST_C1,
+                    across(dx, dy),
+                )
     for dz, dy in plane:
         to = (zl + dz) % 2 * 4 + (y + dy) % 4
         send(bi_s.at[to], bi_r.at[dz * 4 + dy - 1], ST_BI, in_plane(dz, dy))
@@ -190,8 +218,9 @@
     l_dr.wait()
 
     arrived(c1_r, ST_C1)
-    mine = c1_s[core, x * 4 + y].astype(F32)
-    for k in range(31):
+    corner = x * 4 + y
+    mine = c1_s[core, corner].astype(F32) + c1_x[corner].astype(F32)
+    for k in range(15):
         mine = mine + c1_r[k].astype(F32)
     c2_s[...] = mine.astype(BF)
     for dz in (4, 3, 5, 2, 6, 1, 7):
@@ -211,14 +240,11 @@
     arrived(c2_r, ST_C2)
     for k in range(7):
         mine = mine + c2_r[k].astype(F32)
-    rs[core, x * 4 + y] = mine.astype(BF)
-    for dx, dc, dy in third:
-        send(
-            rs.at[core, x * 4 + y],
-            rs.at[core, x * 4 + y],
-            ST_C3,
-            across(dx, dc, dy),
-        )
+    rs[core, corner] = mine.astype(BF)
+    for n, dx in enumerate(reach):
+        for dy in (2, 1, 3, 0):
+            if dx or dy:
+                send(rs.at[core, corner], rs.at[core, corner], ST_C3 + n, across(dx, dy))
     for h in range(2):
         joint[:, 256 * h : 256 * h + 256] = nn(
             bd[:, 384:], d1[:, 256 + 256 * h : 512 + 256 * h]
@@ -228,11 +254,24 @@
         [unpack(si[2 * j], si[2 * j + 1]) for j in range(4)], axis=1
     )
     pre_mid[...] = nt(second_iface, d2[:, :512])
-    arrived(c1_r, ST_C3)
     top = jnp.zeros((R, 64), F32)
-    for j in range(16):
-        v = jnp.concatenate([rs[0, j].astype(F32), rs[1, j].astype(F32)], axis=0)
-        top = top + nt(v.astype(BF), dr[:, 384 * j : 384 * j + 384])
+    for n in (3, 1, 2, 0):
+        g = (x + 4 - reach[n]) % 4
+        arrived(c1_r.at[: 4 if n < 3 else 3], ST_C3 + n)
+        send(rs.at[core, pl.ds(4 * g, 4)], rs.at[core, pl.ds(4 * g, 4)], ST_F + n, sibling)
+    for n in (3, 1, 2, 0):
+        g = (x + 4 - reach[n]) % 4
+        arrived(c1_r.at[:4], ST_F + n)
+        v = jnp.concatenate(
+            [
+                jnp.concatenate(
+                    [rs[0, 4 * g + q].astype(F32), rs[1, 4 * g + q].astype(F32)], axis=0
+                ).astype(BF)
+                for q in range(4)
+            ],
+            axis=1,
+        )
+        top = top + nt(v, dr[:, pl.ds(pl.multiple_of(1536 * g, 128), 1536)])
     d_all[here] = jnp.concatenate([top[:8], top[8:]], axis=1).astype(BF)
     for dz, dy in plane:
         send(d_all.at[here], d_all.at[here], ST_D, in_plane(dz, dy))
@@ -254,7 +293,10 @@
     sent(b2_r, ST_B2)
     sent(c1_r, ST_C1)
     sent(c2_r, ST_C2)
-    sent(c1_r, ST_C3)
+    for n in range(4):
+        sent(c1_r.at[:4], ST_X + n)
+        sent(c1_r.at[: 4 if n < 3 else 3], ST_C3 + n)
+        sent(c1_r.at[:4], ST_F + n)
     sent(b_r, ST_D)
     sent(a_r, ST_E)
 
@@ -300,7 +342,9 @@
             pltpu.VMEM((8, 8, 128), BF),
             pltpu.VMEM((7, 8, 128), BF),
             pltpu.VMEM((2, 16, 8, 384), BF),
-            pltpu.VMEM((31, 8, 384), BF),
+            pltpu.VMEM((16, 8, 384), BF),
+            pltpu.VMEM((16, 8, 384), BF),
+            pltpu.VMEM((15, 8, 384), BF),
             pltpu.VMEM((8, 384), BF),
             pltpu.VMEM((7, 8, 384), BF),
             pltpu.VMEM((2, 16, 8, 384), BF),
@@ -309,6 +353,7 @@
             pltpu.SemaphoreType.DMA((12,)),
             pltpu.SemaphoreType.DMA((N_STAGE,)),
             pltpu.SemaphoreType.DMA((N_STAGE,)),
+            pltpu.SemaphoreType.REGULAR((3,)),
         ],
         compiler_params=pltpu.CompilerParams(
             collective_id=0, has_side_effects=True, vmem_limit_bytes=32 * 1024 * 1024

time: 43.7 us -> 44.5 us (1.018)
  Pallas kernels: 43.6 us -> 44.4 us
    pallas_call x1, Pallas kernels: 42.6 us -> 43.4 us  [per_device(): pl.pallas_call(kernel, out_shape=(jax.ShapeDtypeStruct((R, 1024), BF), ja...]
where the time goes in v3:
time: 44.5 us; the launch traced here: 44.4 us
  Pallas kernels  44.4 us (100%)
    pallas_call x1, Pallas kernels, per_device(): pl.pallas_call(kernel, out_shape=(jax.ShapeDtypeStruct((R, 1024), BF), ja...  43.4 us
    pallas_call x1, Pallas kernels, per_device(): pl.pallas_call(lift, out_shape=jax.ShapeDtypeStruct((R, LEAF, 256), F32),...  0.94 us

profile of v3, /device:TPU:1, one launch (start us, length us, event | category | flops | bytes accessed | tf_op | source)
XLA Modules:
  0.0 44.4 jit_solution(6332530491012620742)
XLA Ops:
  0.0 0.0 copy-start
  0.0 43.4 %shard_map.118 = (bf16[16,1024]{1,0:T(8,128)(2,1)S(1)}, f32[16,16,256]{2,1,0:T(8,128)S(1)}) custom-call(bf16[16,16,256]{2,1,0:T(8,128)(2,1)} %src_h.1, bf16[1024,256]{1,0:T(8,128)(2,1)} %lf_h.1, bf16[4096,256]{1,0:T(8,128)(2,1)} %lp_h.1, bf16[640,1024]{1,0:T(8,128)(2,1)} %bu_h.1, bf16[1024,640]{1,0:T(8,128)(2,1)} %bd_h.1, bf16[256,768]{1,0:T(8,128)(2,1)} %u1_h.1, ...), custom_call_target="tpu_custom_call" | custom-call | tf_op jit(solution)/shard_map/pallas_call | solution.py:320
  43.4 0.0 copy-done
  43.4 0.9 %shard_map.119 = f32[16,16,256]{2,1,0:T(8,128)} custom-call(bf16[16,1024]{1,0:T(8,128)(2,1)S(1)} %get-tuple-element.7.lb_ref, f32[16,16,256]{2,1,0:T(8,128)S(1)} %get-tuple-element.8.part_ref, bf16[1024,256]{1,0:T(8,128)(2,1)S(1)} %copy-done), custom_call_target="tpu_custom_call" | custom-call | tf_op jit(solution)/shard_map/pallas_call | solution.py:362
Async XLA Ops:
  0.0 43.4 %copy-start = (bf16[1024,256]{1,0:T(8,128)(2,1)S(1)}, bf16[1024,256]{1,0:T(8,128)(2,1)}, u32[]{:S(2)}) copy-start(bf16[1024,256]{1,0:T(8,128)(2,1)} %ll_ref.1) | copy-start | bytes 1572868

commit v4 on v3

--- a/solution.py
+++ b/solution.py
@@ -11,9 +11,9 @@
 
 R = 16
 LEAF = 16
-ST_A, ST_AI, ST_B, ST_BI, ST_B2, ST_C1, ST_C2, ST_D, ST_E = range(9)
-ST_X, ST_C3, ST_F = 9, 13, 17
-N_STAGE = 21
+ST_A, ST_AI, ST_B, ST_BI, ST_B2, ST_C1, ST_C2, ST_D, ST_E, ST_UR, ST_DR = range(11)
+ST_C3 = 11
+N_STAGE = 15
 
 
 def nt(x, w):
@@ -31,8 +31,8 @@
     sp, pre_leaf, pre_mid, joint,
     a_s, a_r, ai_s, ai_r,
     b_s, b_r, bi_s, bi_r, si, b2_r,
-    c1_s, c1_x, c1_t, c1_r, c2_s, c2_r, rs,
-    d_all, e_all,
+    c1_s, c1_r, c2_s, c2_r, rs,
+    d_s, d_all, e_all,
     load_sem, send_sem, recv_sem, round_sem,
 ):
     gx = lax.axis_index("gx")
@@ -43,8 +43,8 @@
 
     pairs = (
         (src_h, src), (lf_h, lf), (bu_h.at[384:], bu.at[384:]), (u1_h, u1),
-        (u2_h, u2), (ur_h, ur), (bu_h.at[:384], bu.at[:384]), (lp_h, lp),
-        (bd_h, bd), (d1_h, d1), (d2_h, d2), (dr_h, dr),
+        (u2_h, u2), (ur_h, ur.at[:64]), (bu_h.at[:384], bu.at[:384]), (lp_h, lp),
+        (bd_h, bd), (d1_h, d1), (d2_h, d2), (dr_h, dr.at[:64]),
     )
     loads = [
         pltpu.make_async_copy(h, v, load_sem.at[i]) for i, (h, v) in enumerate(pairs)
@@ -61,12 +61,16 @@
     def in_plane(dz, dy):
         return (gx, (zh * 4 + (zl + dz) % 4) * 4 + (y + dy) % 4)
 
+    def beside(dz, dy):
+        return (sibling[0], (zh * 4 + (zl + dz) % 4) * 4 + (y + dy) % 4)
+
     def along_z(dz):
         return (gx, ((z + dz) % 8) * 4 + y)
 
     x_near = [across(1, 0), across(3, 0)]
     z_near = [along_z(1), along_z(7)]
-    greet = [in_plane(0, 2), in_plane(0, 1), in_plane(0, 3), sibling] + z_near + x_near
+    greet = [in_plane(0, k) for k in (2, 1, 3)] + [beside(0, k) for k in (2, 1, 3, 0)]
+    greet += z_near + x_near
     rounds = (z_near, z_near + x_near, z_near + x_near)
     barrier = pltpu.get_barrier_semaphore()
     for device in greet:
@@ -107,6 +111,12 @@
     cols = lax.broadcasted_iota(jnp.int32, (256, 256), 1)
     pick = ((rows % 16) * 16 + rows // 16 == cols).astype(F32).astype(BF)
     sp[...] = nn(pick, src[...].reshape(R * LEAF, 256)).astype(BF)
+    quarter = lax.broadcasted_iota(jnp.int32, (8, 128), 0) < 4
+    keep = quarter == (lax.broadcasted_iota(jnp.int32, (8, 128), 1) < 64)
+
+    def swap(v):
+        return jnp.where(keep, v, pltpu.roll(pltpu.roll(v, 64, 1), 4, 0))
+
     l_lf.wait()
     lane = lax.broadcasted_iota(jnp.int32, (R, 128), 1)
     low = lax.broadcasted_iota(jnp.int32, (8, 128), 1) < 64
@@ -129,6 +139,8 @@
         blocks.append(jnp.where(lane < 64, f[:16], f[16:]).astype(BF))
     flux = jnp.concatenate(blocks, axis=1)
     pass_on(0)
+    send(ur_h, ur.at[64:], ST_UR, sibling)
+    send(dr_h, dr.at[64:], ST_DR, sibling)
     l_bu.wait()
     box_flux = nt(flux, bu[384:, :]).astype(BF)
     l_u1.wait()
@@ -154,11 +166,17 @@
     second_piece = piece.astype(BF)
     second_flux = nn(second_piece, u2[:, 512:])
     for j in range(8):
-        b_s[2 * j], b_s[2 * j + 1] = pack(second_flux[:, 128 * j : 128 * j + 128])
+        for h in range(2):
+            v = swap(second_flux[8 * h : 8 * h + 8, 128 * j : 128 * j + 128])
+            b_s[h, 2 * j] = v[:4].astype(BF)
+            b_s[h, 2 * j + 1] = v[4:].astype(BF)
     pass_on(3)
-    for dz, dy in plane:
+    for dz, dy in plane + [(0, 0)]:
         to = (zl + dz) % 4 * 4 + (y + dy) % 4
-        send(b_s.at[to], b_r.at[dz * 4 + dy - 1], ST_B, in_plane(dz, dy))
+        slot = dz * 4 + dy - 1
+        if dz or dy:
+            send(b_s.at[core, to], b_r.at[slot], ST_B, in_plane(dz, dy))
+        send(b_s.at[1 - core, to], b_r.at[16 + slot], ST_B, beside(dz, dy))
     second_if = nn(second_piece, u2[:, :512])
     for j in range(4):
         bi_s[2 * j], bi_s[2 * j + 1] = pack(second_if[:, 128 * j : 128 * j + 128])
@@ -168,34 +186,22 @@
 
     arrived(b_r, ST_B)
     here = zl * 4 + y
-    total = b_s[here].astype(F32)
+    total = b_s[core, here].astype(F32)
     for k in range(15):
         total = total + b_r[k].astype(F32)
-    root_piece = jnp.concatenate([total[:, :64], total[:, 64:]], axis=0).astype(BF)
+    other = b_r[15].astype(F32)
+    for k in range(16, 31):
+        other = other + b_r[k].astype(F32)
+    root_piece = swap(jnp.concatenate([total, other], axis=0)).astype(BF)
+    arrived(ur.at[64:], ST_UR)
+    for j in range(16):
+        c1_s[j] = nn(root_piece, ur[:, 384 * j : 384 * j + 384]).astype(BF)
     reach = (2, 1, 3, 0)
-    for n, dx in enumerate(reach):
-        g = (x + dx) % 4
-        t = nn(root_piece, ur[:, pl.ds(pl.multiple_of(1536 * g, 128), 1536)])
-        for q in range(4):
-            c1_s[0, 4 * g + q] = t[:8, 384 * q : 384 * q + 384].astype(BF)
-            c1_s[1, 4 * g + q] = t[8:, 384 * q : 384 * q + 384].astype(BF)
-        send(
-            c1_s.at[1 - core, pl.ds(4 * g, 4)],
-            c1_x.at[pl.ds(4 * g, 4)],
-            ST_X + n,
-            sibling,
-        )
-    for n, dx in enumerate(reach):
-        g = (x + dx) % 4
-        arrived(c1_r.at[:4], ST_X + n)
-        for q in range(4):
-            c1_t[4 * g + q] = (
-                c1_s[core, 4 * g + q].astype(F32) + c1_x[4 * g + q].astype(F32)
-            ).astype(BF)
-        for dy in (2, 1, 3, 0):
+    for dx in reach:
+        for dy in reach:
             if dx or dy:
                 send(
-                    c1_t.at[4 * g + (y + dy) % 4],
+                    c1_s.at[(x + dx) % 4 * 4 + (y + dy) % 4],
                     c1_r.at[dx * 4 + dy - 1],
                     ST_C1,
                     across(dx, dy),
@@ -219,7 +225,7 @@
 
     arrived(c1_r, ST_C1)
     corner = x * 4 + y
-    mine = c1_s[core, corner].astype(F32) + c1_x[corner].astype(F32)
+    mine = c1_s[corner].astype(F32)
     for k in range(15):
         mine = mine + c1_r[k].astype(F32)
     c2_s[...] = mine.astype(BF)
@@ -240,11 +246,11 @@
     arrived(c2_r, ST_C2)
     for k in range(7):
         mine = mine + c2_r[k].astype(F32)
-    rs[core, corner] = mine.astype(BF)
+    rs[corner] = mine.astype(BF)
     for n, dx in enumerate(reach):
         for dy in (2, 1, 3, 0):
             if dx or dy:
-                send(rs.at[core, corner], rs.at[core, corner], ST_C3 + n, across(dx, dy))
+                send(rs.at[corner], rs.at[corner], ST_C3 + n, across(dx, dy))
     for h in range(2):
         joint[:, 256 * h : 256 * h + 256] = nn(
             bd[:, 384:], d1[:, 256 + 256 * h : 512 + 256 * h]
@@ -254,30 +260,41 @@
         [unpack(si[2 * j], si[2 * j + 1]) for j in range(4)], axis=1
     )
     pre_mid[...] = nt(second_iface, d2[:, :512])
-    top = jnp.zeros((R, 64), F32)
+    arrived(dr.at[64:], ST_DR)
+    top = jnp.zeros((8, 128), F32)
     for n in (3, 1, 2, 0):
         g = (x + 4 - reach[n]) % 4
         arrived(c1_r.at[: 4 if n < 3 else 3], ST_C3 + n)
-        send(rs.at[core, pl.ds(4 * g, 4)], rs.at[core, pl.ds(4 * g, 4)], ST_F + n, sibling)
-    for n in (3, 1, 2, 0):
-        g = (x + 4 - reach[n]) % 4
-        arrived(c1_r.at[:4], ST_F + n)
-        v = jnp.concatenate(
-            [
-                jnp.concatenate(
-                    [rs[0, 4 * g + q].astype(F32), rs[1, 4 * g + q].astype(F32)], axis=0
-                ).astype(BF)
-                for q in range(4)
-            ],
-            axis=1,
-        )
+        v = jnp.concatenate([rs[4 * g + q] for q in range(4)], axis=1)
         top = top + nt(v, dr[:, pl.ds(pl.multiple_of(1536 * g, 128), 1536)])
-    d_all[here] = jnp.concatenate([top[:8], top[8:]], axis=1).astype(BF)
-    for dz, dy in plane:
-        send(d_all.at[here], d_all.at[here], ST_D, in_plane(dz, dy))
+    top = swap(top)
+    d_all[core, here] = top[:4].astype(BF)
+    d_s[...] = top[4:].astype(BF)
+    for dz, dy in plane + [(0, 0)]:
+        if dz or dy:
+            send(d_all.at[core, here], d_all.at[core, here], ST_D, in_plane(dz, dy))
+        send(d_s, d_all.at[core, here], ST_D, beside(dz, dy))
     arrived(b_r, ST_D)
     top_bound = jnp.concatenate(
-        [unpack(d_all[2 * j], d_all[2 * j + 1]) for j in range(8)], axis=1
+        [
+            jnp.concatenate(
+                [
+                    swap(
+                        jnp.concatenate(
+                            [
+                                d_all[h, 2 * j].astype(F32),
+                                d_all[h, 2 * j + 1].astype(F32),
+                            ],
+                            axis=0,
+                        )
+                    )
+                    for h in range(2)
+                ],
+                axis=0,
+            ).astype(BF)
+            for j in range(8)
+        ],
+        axis=1,
     )
     e_all[y] = (pre_mid[...] + nt(top_bound, d2[:, 512:])).astype(BF)
     for k in (2, 1, 3):
@@ -294,9 +311,9 @@
     sent(c1_r, ST_C1)
     sent(c2_r, ST_C2)
     for n in range(4):
-        sent(c1_r.at[:4], ST_X + n)
         sent(c1_r.at[: 4 if n < 3 else 3], ST_C3 + n)
-        sent(c1_r.at[:4], ST_F + n)
+    sent(ur.at[64:], ST_UR)
+    sent(dr.at[64:], ST_DR)
     sent(b_r, ST_D)
     sent(a_r, ST_E)
 
@@ -325,7 +342,8 @@
         ),
         in_specs=[pl.BlockSpec(memory_space=pltpu.HBM)] * 11,
         out_specs=(vmem, vmem),
-        scratch_shapes=[pltpu.VMEM(a.shape, BF) for a in args]
+        scratch_shapes=[pltpu.VMEM(a.shape, BF) for a in args[:-2]]
+        + [pltpu.VMEM((128, 6144), BF)] * 2
         + [
             pltpu.VMEM((256, 256), BF),
             pltpu.VMEM((16, 1024), F32),
@@ -335,20 +353,19 @@
             pltpu.VMEM((3, 16, 128), BF),
             pltpu.VMEM((16, 256), BF),
             pltpu.VMEM((3, 16, 256), BF),
-            pltpu.VMEM((16, 8, 128), BF),
-            pltpu.VMEM((15, 8, 128), BF),
+            pltpu.VMEM((2, 16, 4, 128), BF),
+            pltpu.VMEM((31, 4, 128), BF),
             pltpu.VMEM((8, 8, 128), BF),
             pltpu.VMEM((15, 8, 128), BF),
             pltpu.VMEM((8, 8, 128), BF),
             pltpu.VMEM((7, 8, 128), BF),
-            pltpu.VMEM((2, 16, 8, 384), BF),
-            pltpu.VMEM((16, 8, 384), BF),
             pltpu.VMEM((16, 8, 384), BF),
             pltpu.VMEM((15, 8, 384), BF),
             pltpu.VMEM((8, 384), BF),
             pltpu.VMEM((7, 8, 384), BF),
-            pltpu.VMEM((2, 16, 8, 384), BF),
-            pltpu.VMEM((16, 8, 128), BF),
+            pltpu.VMEM((16, 8, 384), BF),
+            pltpu.VMEM((4, 128), BF),
+            pltpu.VMEM((2, 16, 4, 128), BF),
             pltpu.VMEM((4, 16, 128), BF),
             pltpu.SemaphoreType.DMA((12,)),
             pltpu.SemaphoreType.DMA((N_STAGE,)),

time: 44.5 us -> 43.8 us (0.984)
  Pallas kernels: 44.4 us -> 43.7 us
    pallas_call x1, Pallas kernels: 43.4 us -> 42.7 us  [per_device(): pl.pallas_call(kernel, out_shape=(jax.ShapeDtypeStruct((R, 1024), BF), ja...]
where the time goes in v4:
time: 43.8 us; the launch traced here: 43.7 us
  Pallas kernels  43.7 us (100%)
    pallas_call x1, Pallas kernels, per_device(): pl.pallas_call(kernel, out_shape=(jax.ShapeDtypeStruct((R, 1024), BF), ja...  42.7 us
    pallas_call x1, Pallas kernels, per_device(): pl.pallas_call(lift, out_shape=jax.ShapeDtypeStruct((R, LEAF, 256), F32),...  0.94 us

profile of v4, /device:TPU:1, one launch (start us, length us, event | category | flops | bytes accessed | tf_op | source)
XLA Modules:
  0.0 43.7 jit_solution(8848203859771033999)
XLA Ops:
  0.0 0.0 copy-start
  0.0 42.7 %shard_map.118 = (bf16[16,1024]{1,0:T(8,128)(2,1)S(1)}, f32[16,16,256]{2,1,0:T(8,128)S(1)}) custom-call(bf16[16,16,256]{2,1,0:T(8,128)(2,1)} %src_h.1, bf16[1024,256]{1,0:T(8,128)(2,1)} %lf_h.1, bf16[4096,256]{1,0:T(8,128)(2,1)} %lp_h.1, bf16[640,1024]{1,0:T(8,128)(2,1)} %bu_h.1, bf16[1024,640]{1,0:T(8,128)(2,1)} %bd_h.1, bf16[256,768]{1,0:T(8,128)(2,1)} %u1_h.1, ...), custom_call_target="tpu_custom_call" | custom-call | tf_op jit(solution)/shard_map/pallas_call | solution.py:337
  42.7 0.0 copy-done
  42.7 0.9 %shard_map.119 = f32[16,16,256]{2,1,0:T(8,128)} custom-call(bf16[16,1024]{1,0:T(8,128)(2,1)S(1)} %get-tuple-element.7.lb_ref, f32[16,16,256]{2,1,0:T(8,128)S(1)} %get-tuple-element.8.part_ref, bf16[1024,256]{1,0:T(8,128)(2,1)S(1)} %copy-done), custom_call_target="tpu_custom_call" | custom-call | tf_op jit(solution)/shard_map/pallas_call | solution.py:379
Async XLA Ops:
  0.0 42.7 %copy-start = (bf16[1024,256]{1,0:T(8,128)(2,1)S(1)}, bf16[1024,256]{1,0:T(8,128)(2,1)}, u32[]{:S(2)}) copy-start(bf16[1024,256]{1,0:T(8,128)(2,1)} %ll_ref.1) | copy-start | bytes 1572868

commit v5 on v4

--- a/solution.py
+++ b/solution.py
@@ -12,8 +12,8 @@
 R = 16
 LEAF = 16
 ST_A, ST_AI, ST_B, ST_BI, ST_B2, ST_C1, ST_C2, ST_D, ST_E, ST_UR, ST_DR = range(11)
-ST_C3 = 11
-N_STAGE = 15
+ST_C3, ST_B3, ST_BX, ST_DX = 11, 15, 16, 17
+N_STAGE = 18
 
 
 def nt(x, w):
@@ -30,7 +30,7 @@
     src, lf, lp, bu, bd, u1, d1, u2, d2, ur, dr,
     sp, pre_leaf, pre_mid, joint,
     a_s, a_r, ai_s, ai_r,
-    b_s, b_r, bi_s, bi_r, si, b2_r,
+    b_s, b_r, bx_s, bx_r, bi_s, bi_r, b2_s, b2_r, si,
     c1_s, c1_r, c2_s, c2_r, rs,
     d_s, d_all, e_all,
     load_sem, send_sem, recv_sem, round_sem,
@@ -61,16 +61,12 @@
     def in_plane(dz, dy):
         return (gx, (zh * 4 + (zl + dz) % 4) * 4 + (y + dy) % 4)
 
-    def beside(dz, dy):
-        return (sibling[0], (zh * 4 + (zl + dz) % 4) * 4 + (y + dy) % 4)
-
     def along_z(dz):
         return (gx, ((z + dz) % 8) * 4 + y)
 
     x_near = [across(1, 0), across(3, 0)]
     z_near = [along_z(1), along_z(7)]
-    greet = [in_plane(0, k) for k in (2, 1, 3)] + [beside(0, k) for k in (2, 1, 3, 0)]
-    greet += z_near + x_near
+    greet = [in_plane(0, k) for k in (2, 1, 3)] + [sibling] + z_near + x_near
     rounds = (z_near, z_near + x_near, z_near + x_near)
     barrier = pltpu.get_barrier_semaphore()
     for device in greet:
@@ -119,20 +115,6 @@
 
     l_lf.wait()
     lane = lax.broadcasted_iota(jnp.int32, (R, 128), 1)
-    low = lax.broadcasted_iota(jnp.int32, (8, 128), 1) < 64
-
-    def pack(v):
-        up, down = v[:8], v[8:]
-        first = jnp.where(low, up, pltpu.roll(down, 64, 1))
-        second = jnp.where(low, pltpu.roll(up, 64, 1), down)
-        return first.astype(BF), second.astype(BF)
-
-    def unpack(first, second):
-        first, second = first.astype(F32), second.astype(F32)
-        up = jnp.where(low, first, pltpu.roll(second, 64, 1))
-        down = jnp.where(low, pltpu.roll(first, 64, 1), second)
-        return jnp.concatenate([up, down], axis=0).astype(BF)
-
     blocks = []
     for m in range(8):
         f = nt(sp[32 * m : 32 * m + 32, :], lf[128 * m : 128 * m + 128, :])
@@ -168,31 +150,33 @@
     for j in range(8):
         for h in range(2):
             v = swap(second_flux[8 * h : 8 * h + 8, 128 * j : 128 * j + 128])
-            b_s[h, 2 * j] = v[:4].astype(BF)
-            b_s[h, 2 * j + 1] = v[4:].astype(BF)
+            b_s[2 * j, h] = v[:4].astype(BF)
+            b_s[2 * j + 1, h] = v[4:].astype(BF)
     pass_on(3)
-    for dz, dy in plane + [(0, 0)]:
+    for dz, dy in plane:
         to = (zl + dz) % 4 * 4 + (y + dy) % 4
-        slot = dz * 4 + dy - 1
-        if dz or dy:
-            send(b_s.at[core, to], b_r.at[slot], ST_B, in_plane(dz, dy))
-        send(b_s.at[1 - core, to], b_r.at[16 + slot], ST_B, beside(dz, dy))
+        send(b_s.at[to], b_r.at[dz * 4 + dy - 1], ST_B, in_plane(dz, dy))
     second_if = nn(second_piece, u2[:, :512])
     for j in range(4):
-        bi_s[2 * j], bi_s[2 * j + 1] = pack(second_if[:, 128 * j : 128 * j + 128])
+        bi_s[j] = second_if[:, 128 * j : 128 * j + 128].astype(BF)
+    for k in (2, 1, 3):
+        send(bi_s.at[(y + k) % 4], bi_r.at[k - 1], ST_BI, in_plane(0, k))
     l_bi.wait()
     box_if = nt(flux, bu[:384, :]).astype(BF)
     l_ur.wait()
 
     arrived(b_r, ST_B)
     here = zl * 4 + y
-    total = b_s[core, here].astype(F32)
-    for k in range(15):
-        total = total + b_r[k].astype(F32)
-    other = b_r[15].astype(F32)
-    for k in range(16, 31):
-        other = other + b_r[k].astype(F32)
-    root_piece = swap(jnp.concatenate([total, other], axis=0)).astype(BF)
+    for h in range(2):
+        total = b_s[here, h].astype(F32)
+        for k in range(15):
+            total = total + b_r[k, h].astype(F32)
+        bx_s[h] = total.astype(BF)
+    send(bx_s.at[1 - core], bx_r, ST_BX, sibling)
+    arrived(bx_r, ST_BX)
+    root_piece = swap(
+        jnp.concatenate([bx_s[core].astype(F32), bx_r[...].astype(F32)], axis=0)
+    ).astype(BF)
     arrived(ur.at[64:], ST_UR)
     for j in range(16):
         c1_s[j] = nn(root_piece, ur[:, 384 * j : 384 * j + 384]).astype(BF)
@@ -206,9 +190,13 @@
                     ST_C1,
                     across(dx, dy),
                 )
-    for dz, dy in plane:
-        to = (zl + dz) % 2 * 4 + (y + dy) % 4
-        send(bi_s.at[to], bi_r.at[dz * 4 + dy - 1], ST_BI, in_plane(dz, dy))
+    arrived(bi_r, ST_BI)
+    block = bi_s[y].astype(F32)
+    for k in range(3):
+        block = block + bi_r[k].astype(F32)
+    b2_s[...] = block.astype(BF)
+    for dz in (2, 3, 1):
+        send(b2_s, b2_r.at[dz - 1], ST_B2, in_plane(dz, 0))
     l_lp.wait()
     for l in range(LEAF):
         part[l] = nn(sp[16 * l : 16 * l + 16, :], lp[256 * l : 256 * l + 256, :])
@@ -231,17 +219,12 @@
     c2_s[...] = mine.astype(BF)
     for dz in (4, 3, 5, 2, 6, 1, 7):
         send(c2_s, c2_r.at[dz - 1], ST_C2, along_z(dz))
-    arrived(bi_r, ST_BI)
-    own = zl % 2 * 4 + y
-    total = bi_s[own].astype(F32)
-    for k in range(15):
-        total = total + bi_r[k].astype(F32)
-    si[own] = total.astype(BF)
-    flip = zl + 1 - zl % 2 * 2
-    for dy in (2, 1, 3, 0):
-        send(si.at[own], si.at[own], ST_B2, (gx, (zh * 4 + flip) * 4 + (y + dy) % 4))
-    for dy in (2, 1, 3):
-        send(si.at[own], si.at[own], ST_B2, in_plane(0, dy))
+    arrived(b2_r, ST_B2)
+    for k in range(3):
+        block = block + b2_r[k].astype(F32)
+    si[y] = block.astype(BF)
+    for k in (2, 1, 3):
+        send(si.at[y], si.at[y], ST_B3, in_plane(0, k))
 
     arrived(c2_r, ST_C2)
     for k in range(7):
@@ -255,10 +238,8 @@
         joint[:, 256 * h : 256 * h + 256] = nn(
             bd[:, 384:], d1[:, 256 + 256 * h : 512 + 256 * h]
         ).astype(BF)
-    arrived(b2_r, ST_B2)
-    second_iface = jnp.concatenate(
-        [unpack(si[2 * j], si[2 * j + 1]) for j in range(4)], axis=1
-    )
+    arrived(bi_r, ST_B3)
+    second_iface = jnp.concatenate([si[j] for j in range(4)], axis=1)
     pre_mid[...] = nt(second_iface, d2[:, :512])
     arrived(dr.at[64:], ST_DR)
     top = jnp.zeros((8, 128), F32)
@@ -268,12 +249,12 @@
         v = jnp.concatenate([rs[4 * g + q] for q in range(4)], axis=1)
         top = top + nt(v, dr[:, pl.ds(pl.multiple_of(1536 * g, 128), 1536)])
     top = swap(top)
-    d_all[core, here] = top[:4].astype(BF)
+    d_all[here, core] = top[:4].astype(BF)
     d_s[...] = top[4:].astype(BF)
-    for dz, dy in plane + [(0, 0)]:
-        if dz or dy:
-            send(d_all.at[core, here], d_all.at[core, here], ST_D, in_plane(dz, dy))
-        send(d_s, d_all.at[core, here], ST_D, beside(dz, dy))
+    send(d_s, d_all.at[here, core], ST_DX, sibling)
+    arrived(d_s, ST_DX)
+    for dz, dy in plane:
+        send(d_all.at[here], d_all.at[here], ST_D, in_plane(dz, dy))
     arrived(b_r, ST_D)
     top_bound = jnp.concatenate(
         [
@@ -282,8 +263,8 @@
                     swap(
                         jnp.concatenate(
                             [
-                                d_all[h, 2 * j].astype(F32),
-                                d_all[h, 2 * j + 1].astype(F32),
+                                d_all[2 * j, h].astype(F32),
+                                d_all[2 * j + 1, h].astype(F32),
                             ],
                             axis=0,
                         )
@@ -308,6 +289,9 @@
     sent(b_r, ST_B)
     sent(bi_r, ST_BI)
     sent(b2_r, ST_B2)
+    sent(bi_r, ST_B3)
+    sent(bx_r, ST_BX)
+    sent(d_s, ST_DX)
     sent(c1_r, ST_C1)
     sent(c2_r, ST_C2)
     for n in range(4):
@@ -353,19 +337,22 @@
             pltpu.VMEM((3, 16, 128), BF),
             pltpu.VMEM((16, 256), BF),
             pltpu.VMEM((3, 16, 256), BF),
-            pltpu.VMEM((2, 16, 4, 128), BF),
-            pltpu.VMEM((31, 4, 128), BF),
-            pltpu.VMEM((8, 8, 128), BF),
-            pltpu.VMEM((15, 8, 128), BF),
-            pltpu.VMEM((8, 8, 128), BF),
-            pltpu.VMEM((7, 8, 128), BF),
+            pltpu.VMEM((16, 2, 4, 128), BF),
+            pltpu.VMEM((15, 2, 4, 128), BF),
+            pltpu.VMEM((2, 4, 128), BF),
+            pltpu.VMEM((4, 128), BF),
+            pltpu.VMEM((4, 16, 128), BF),
+            pltpu.VMEM((3, 16, 128), BF),
+            pltpu.VMEM((16, 128), BF),
+            pltpu.VMEM((3, 16, 128), BF),
+            pltpu.VMEM((4, 16, 128), BF),
             pltpu.VMEM((16, 8, 384), BF),
             pltpu.VMEM((15, 8, 384), BF),
             pltpu.VMEM((8, 384), BF),
             pltpu.VMEM((7, 8, 384), BF),
             pltpu.VMEM((16, 8, 384), BF),
             pltpu.VMEM((4, 128), BF),
-            pltpu.VMEM((2, 16, 4, 128), BF),
+            pltpu.VMEM((16, 2, 4, 128), BF),
             pltpu.VMEM((4, 16, 128), BF),
             pltpu.SemaphoreType.DMA((12,)),
             pltpu.SemaphoreType.DMA((N_STAGE,)),

time: 43.8 us -> 44.2 us (level)
  no operation moved by 1% of the time
where the time goes in v5:
time: 44.2 us; the launch traced here: 44.1 us
  Pallas kernels  44.1 us (100%)
    pallas_call x1, Pallas kernels, per_device(): pl.pallas_call(kernel, out_shape=(jax.ShapeDtypeStruct((R, 1024), BF), ja...  43.1 us
    pallas_call x1, Pallas kernels, per_device(): pl.pallas_call(lift, out_shape=jax.ShapeDtypeStruct((R, LEAF, 256), F32),...  0.94 us

profile of v5, /device:TPU:1, one launch (start us, length us, event | category | flops | bytes accessed | tf_op | source)
XLA Modules:
  0.0 44.1 jit_solution(18143736064063106422)
XLA Ops:
  0.0 0.0 copy-start
  0.0 43.1 %shard_map.118 = (bf16[16,1024]{1,0:T(8,128)(2,1)S(1)}, f32[16,16,256]{2,1,0:T(8,128)S(1)}) custom-call(bf16[16,16,256]{2,1,0:T(8,128)(2,1)} %src_h.1, bf16[1024,256]{1,0:T(8,128)(2,1)} %lf_h.1, bf16[4096,256]{1,0:T(8,128)(2,1)} %lp_h.1, bf16[640,1024]{1,0:T(8,128)(2,1)} %bu_h.1, bf16[1024,640]{1,0:T(8,128)(2,1)} %bd_h.1, bf16[256,768]{1,0:T(8,128)(2,1)} %u1_h.1, ...), custom_call_target="tpu_custom_call" | custom-call | tf_op jit(solution)/shard_map/pallas_call | solution.py:321
  43.1 0.0 copy-done
  43.2 0.9 %shard_map.119 = f32[16,16,256]{2,1,0:T(8,128)} custom-call(bf16[16,1024]{1,0:T(8,128)(2,1)S(1)} %get-tuple-element.7.lb_ref, f32[16,16,256]{2,1,0:T(8,128)S(1)} %get-tuple-element.8.part_ref, bf16[1024,256]{1,0:T(8,128)(2,1)S(1)} %copy-done), custom_call_target="tpu_custom_call" | custom-call | tf_op jit(solution)/shard_map/pallas_call | solution.py:366
Async XLA Ops:
  0.0 43.1 %copy-start = (bf16[1024,256]{1,0:T(8,128)(2,1)S(1)}, bf16[1024,256]{1,0:T(8,128)(2,1)}, u32[]{:S(2)}) copy-start(bf16[1024,256]{1,0:T(8,128)(2,1)} %ll_ref.1) | copy-start | bytes 1572868

commit v6 on v5

--- a/solution.py
+++ b/solution.py
@@ -12,7 +12,7 @@
 R = 16
 LEAF = 16
 ST_A, ST_AI, ST_B, ST_BI, ST_B2, ST_C1, ST_C2, ST_D, ST_E, ST_UR, ST_DR = range(11)
-ST_C3, ST_B3, ST_BX, ST_DX = 11, 15, 16, 17
+ST_C3, ST_B3, ST_U2, ST_D2 = 11, 15, 16, 17
 N_STAGE = 18
 
 
@@ -30,9 +30,9 @@
     src, lf, lp, bu, bd, u1, d1, u2, d2, ur, dr,
     sp, pre_leaf, pre_mid, joint,
     a_s, a_r, ai_s, ai_r,
-    b_s, b_r, bx_s, bx_r, bi_s, bi_r, b2_s, b2_r, si,
+    b_s, b_r, bi_s, bi_r, b2_s, b2_r, si,
     c1_s, c1_r, c2_s, c2_r, rs,
-    d_s, d_all, e_all,
+    d_all, e_s, e_all,
     load_sem, send_sem, recv_sem, round_sem,
 ):
     gx = lax.axis_index("gx")
@@ -43,8 +43,8 @@
 
     pairs = (
         (src_h, src), (lf_h, lf), (bu_h.at[384:], bu.at[384:]), (u1_h, u1),
-        (u2_h, u2), (ur_h, ur.at[:64]), (bu_h.at[:384], bu.at[:384]), (lp_h, lp),
-        (bd_h, bd), (d1_h, d1), (d2_h, d2), (dr_h, dr.at[:64]),
+        (u2_h, u2.at[:128]), (ur_h, ur.at[:64]), (bu_h.at[:384], bu.at[:384]), (lp_h, lp),
+        (bd_h, bd), (d1_h, d1), (d2_h, d2.at[:128]), (dr_h, dr.at[:64]),
     )
     loads = [
         pltpu.make_async_copy(h, v, load_sem.at[i]) for i, (h, v) in enumerate(pairs)
@@ -61,12 +61,16 @@
     def in_plane(dz, dy):
         return (gx, (zh * 4 + (zl + dz) % 4) * 4 + (y + dy) % 4)
 
+    def beside(dy):
+        return (sibling[0], z * 4 + (y + dy) % 4)
+
     def along_z(dz):
         return (gx, ((z + dz) % 8) * 4 + y)
 
     x_near = [across(1, 0), across(3, 0)]
     z_near = [along_z(1), along_z(7)]
-    greet = [in_plane(0, k) for k in (2, 1, 3)] + [sibling] + z_near + x_near
+    greet = [in_plane(0, k) for k in (2, 1, 3)] + [beside(k) for k in (2, 1, 3, 0)]
+    greet += z_near + x_near
     rounds = (z_near, z_near + x_near, z_near + x_near)
     barrier = pltpu.get_barrier_semaphore()
     for device in greet:
@@ -107,11 +111,13 @@
     cols = lax.broadcasted_iota(jnp.int32, (256, 256), 1)
     pick = ((rows % 16) * 16 + rows // 16 == cols).astype(F32).astype(BF)
     sp[...] = nn(pick, src[...].reshape(R * LEAF, 256)).astype(BF)
-    quarter = lax.broadcasted_iota(jnp.int32, (8, 128), 0) < 4
-    keep = quarter == (lax.broadcasted_iota(jnp.int32, (8, 128), 1) < 64)
-
-    def swap(v):
-        return jnp.where(keep, v, pltpu.roll(pltpu.roll(v, 64, 1), 4, 0))
+    low = lax.broadcasted_iota(jnp.int32, (8, 128), 1) < 64
+
+    def weave(a, b):
+        return (
+            jnp.where(low, a, pltpu.roll(b, 64, 1)),
+            jnp.where(low, pltpu.roll(a, 64, 1), b),
+        )
 
     l_lf.wait()
     lane = lax.broadcasted_iota(jnp.int32, (R, 128), 1)
@@ -121,7 +127,9 @@
         blocks.append(jnp.where(lane < 64, f[:16], f[16:]).astype(BF))
     flux = jnp.concatenate(blocks, axis=1)
     pass_on(0)
+    send(u2_h, u2.at[128:], ST_U2, sibling)
     send(ur_h, ur.at[64:], ST_UR, sibling)
+    send(d2_h, d2.at[128:], ST_D2, sibling)
     send(dr_h, dr.at[64:], ST_DR, sibling)
     l_bu.wait()
     box_flux = nt(flux, bu[384:, :]).astype(BF)
@@ -130,9 +138,12 @@
         l.start()
     first_flux = nn(box_flux, u1[:, 256:])
     for j in range(4):
-        a_s[j] = first_flux[:, 128 * j : 128 * j + 128].astype(BF)
-    for k in (2, 1, 3):
-        send(a_s.at[(y + k) % 4], a_r.at[k - 1], ST_A, in_plane(0, k))
+        for h in range(2):
+            a_s[h, j] = first_flux[8 * h : 8 * h + 8, 128 * j : 128 * j + 128].astype(BF)
+    for k in (2, 1, 3, 0):
+        if k:
+            send(a_s.at[core, (y + k) % 4], a_r.at[k - 1], ST_A, in_plane(0, k))
+        send(a_s.at[1 - core, (y + k) % 4], a_r.at[3 + k], ST_A, beside(k))
     pass_on(1)
     first_if = nn(box_flux, u1[:, :256])
     ai_s[...] = first_if.astype(BF)
@@ -142,23 +153,29 @@
     l_u2.wait()
 
     arrived(a_r, ST_A)
-    piece = a_s[y].astype(F32)
+    piece = a_s[core, y].astype(F32)
+    other = a_r[3].astype(F32)
     for k in range(3):
         piece = piece + a_r[k].astype(F32)
-    second_piece = piece.astype(BF)
-    second_flux = nn(second_piece, u2[:, 512:])
+        other = other + a_r[4 + k].astype(F32)
+    piece, other = piece.astype(BF), other.astype(BF)
+    arrived(u2.at[128:], ST_U2)
+    mine2 = nn(piece, u2[:128, 512:])
+    other2 = nn(other, u2[128:, 512:])
     for j in range(8):
-        for h in range(2):
-            v = swap(second_flux[8 * h : 8 * h + 8, 128 * j : 128 * j + 128])
-            b_s[2 * j, h] = v[:4].astype(BF)
-            b_s[2 * j + 1, h] = v[4:].astype(BF)
+        cut = slice(128 * j, 128 * j + 128)
+        even, odd = weave(mine2[:, cut], other2[:, cut])
+        b_s[2 * j] = even.astype(BF)
+        b_s[2 * j + 1] = odd.astype(BF)
     pass_on(3)
     for dz, dy in plane:
         to = (zl + dz) % 4 * 4 + (y + dy) % 4
         send(b_s.at[to], b_r.at[dz * 4 + dy - 1], ST_B, in_plane(dz, dy))
-    second_if = nn(second_piece, u2[:, :512])
+    mine_if = nn(piece, u2[:128, :512])
+    other_if = nn(other, u2[128:, :512])
     for j in range(4):
-        bi_s[j] = second_if[:, 128 * j : 128 * j + 128].astype(BF)
+        bi_s[j, 0] = mine_if[:, 128 * j : 128 * j + 128].astype(BF)
+        bi_s[j, 1] = other_if[:, 128 * j : 128 * j + 128].astype(BF)
     for k in (2, 1, 3):
         send(bi_s.at[(y + k) % 4], bi_r.at[k - 1], ST_BI, in_plane(0, k))
     l_bi.wait()
@@ -167,16 +184,10 @@
 
     arrived(b_r, ST_B)
     here = zl * 4 + y
-    for h in range(2):
-        total = b_s[here, h].astype(F32)
-        for k in range(15):
-            total = total + b_r[k, h].astype(F32)
-        bx_s[h] = total.astype(BF)
-    send(bx_s.at[1 - core], bx_r, ST_BX, sibling)
-    arrived(bx_r, ST_BX)
-    root_piece = swap(
-        jnp.concatenate([bx_s[core].astype(F32), bx_r[...].astype(F32)], axis=0)
-    ).astype(BF)
+    total = b_s[here].astype(F32)
+    for k in range(15):
+        total = total + b_r[k].astype(F32)
+    root_piece = total.astype(BF)
     arrived(ur.at[64:], ST_UR)
     for j in range(16):
         c1_s[j] = nn(root_piece, ur[:, 384 * j : 384 * j + 384]).astype(BF)
@@ -239,8 +250,10 @@
             bd[:, 384:], d1[:, 256 + 256 * h : 512 + 256 * h]
         ).astype(BF)
     arrived(bi_r, ST_B3)
-    second_iface = jnp.concatenate([si[j] for j in range(4)], axis=1)
-    pre_mid[...] = nt(second_iface, d2[:, :512])
+    arrived(d2.at[128:], ST_D2)
+    for h in range(2):
+        second_iface = jnp.concatenate([si[j, h] for j in range(4)], axis=1)
+        pre_mid[h] = nt(second_iface, d2[128 * h : 128 * h + 128, :512])
     arrived(dr.at[64:], ST_DR)
     top = jnp.zeros((8, 128), F32)
     for n in (3, 1, 2, 0):
@@ -248,40 +261,35 @@
         arrived(c1_r.at[: 4 if n < 3 else 3], ST_C3 + n)
         v = jnp.concatenate([rs[4 * g + q] for q in range(4)], axis=1)
         top = top + nt(v, dr[:, pl.ds(pl.multiple_of(1536 * g, 128), 1536)])
-    top = swap(top)
-    d_all[here, core] = top[:4].astype(BF)
-    d_s[...] = top[4:].astype(BF)
-    send(d_s, d_all.at[here, core], ST_DX, sibling)
-    arrived(d_s, ST_DX)
+    d_all[here] = top.astype(BF)
     for dz, dy in plane:
         send(d_all.at[here], d_all.at[here], ST_D, in_plane(dz, dy))
     arrived(b_r, ST_D)
-    top_bound = jnp.concatenate(
+    pairs = [
+        weave(d_all[2 * j].astype(F32), d_all[2 * j + 1].astype(F32)) for j in range(8)
+    ]
+    mids = []
+    for h in range(2):
+        bound = jnp.concatenate([p[h] for p in pairs], axis=1).astype(BF)
+        mids.append(
+            (pre_mid[h] + nt(bound, d2[128 * h : 128 * h + 128, 512:])).astype(BF)
+        )
+    e_all[core, y] = mids[0]
+    e_s[...] = mids[1]
+    for k in (2, 1, 3, 0):
+        if k:
+            send(e_all.at[core, y], e_all.at[core, y], ST_E, in_plane(0, k))
+        send(e_s, e_all.at[core, y], ST_E, beside(k))
+    arrived(a_r, ST_E)
+    mid_bound = jnp.concatenate(
         [
             jnp.concatenate(
-                [
-                    swap(
-                        jnp.concatenate(
-                            [
-                                d_all[2 * j, h].astype(F32),
-                                d_all[2 * j + 1, h].astype(F32),
-                            ],
-                            axis=0,
-                        )
-                    )
-                    for h in range(2)
-                ],
-                axis=0,
+                [e_all[0, j].astype(F32), e_all[1, j].astype(F32)], axis=0
             ).astype(BF)
-            for j in range(8)
+            for j in range(4)
         ],
         axis=1,
     )
-    e_all[y] = (pre_mid[...] + nt(top_bound, d2[:, 512:])).astype(BF)
-    for k in (2, 1, 3):
-        send(e_all.at[y], e_all.at[y], ST_E, in_plane(0, k))
-    arrived(a_r, ST_E)
-    mid_bound = jnp.concatenate([e_all[j] for j in range(4)], axis=1)
     lb_ref[...] = (pre_leaf[...] + nt(mid_bound, joint[...])).astype(BF)
 
     sent(a_r, ST_A)
@@ -290,8 +298,8 @@
     sent(bi_r, ST_BI)
     sent(b2_r, ST_B2)
     sent(bi_r, ST_B3)
-    sent(bx_r, ST_BX)
-    sent(d_s, ST_DX)
+    sent(u2.at[128:], ST_U2)
+    sent(d2.at[128:], ST_D2)
     sent(c1_r, ST_C1)
     sent(c2_r, ST_C2)
     for n in range(4):
@@ -326,34 +334,32 @@
         ),
         in_specs=[pl.BlockSpec(memory_space=pltpu.HBM)] * 11,
         out_specs=(vmem, vmem),
-        scratch_shapes=[pltpu.VMEM(a.shape, BF) for a in args[:-2]]
-        + [pltpu.VMEM((128, 6144), BF)] * 2
+        scratch_shapes=[pltpu.VMEM(a.shape, BF) for a in args[:-4]]
+        + [pltpu.VMEM((2 * a.shape[0], a.shape[1]), BF) for a in args[-4:]]
         + [
             pltpu.VMEM((256, 256), BF),
             pltpu.VMEM((16, 1024), F32),
-            pltpu.VMEM((16, 128), F32),
+            pltpu.VMEM((2, 8, 128), F32),
             pltpu.VMEM((1024, 512), BF),
-            pltpu.VMEM((4, 16, 128), BF),
-            pltpu.VMEM((3, 16, 128), BF),
+            pltpu.VMEM((2, 4, 8, 128), BF),
+            pltpu.VMEM((7, 8, 128), BF),
             pltpu.VMEM((16, 256), BF),
             pltpu.VMEM((3, 16, 256), BF),
-            pltpu.VMEM((16, 2, 4, 128), BF),
-            pltpu.VMEM((15, 2, 4, 128), BF),
-            pltpu.VMEM((2, 4, 128), BF),
-            pltpu.VMEM((4, 128), BF),
-            pltpu.VMEM((4, 16, 128), BF),
-            pltpu.VMEM((3, 16, 128), BF),
-            pltpu.VMEM((16, 128), BF),
-            pltpu.VMEM((3, 16, 128), BF),
-            pltpu.VMEM((4, 16, 128), BF),
+            pltpu.VMEM((16, 8, 128), BF),
+            pltpu.VMEM((15, 8, 128), BF),
+            pltpu.VMEM((4, 2, 8, 128), BF),
+            pltpu.VMEM((3, 2, 8, 128), BF),
+            pltpu.VMEM((2, 8, 128), BF),
+            pltpu.VMEM((3, 2, 8, 128), BF),
+            pltpu.VMEM((4, 2, 8, 128), BF),
             pltpu.VMEM((16, 8, 384), BF),
             pltpu.VMEM((15, 8, 384), BF),
             pltpu.VMEM((8, 384), BF),
             pltpu.VMEM((7, 8, 384), BF),
             pltpu.VMEM((16, 8, 384), BF),
-            pltpu.VMEM((4, 128), BF),
-            pltpu.VMEM((16, 2, 4, 128), BF),
-            pltpu.VMEM((4, 16, 128), BF),
+            pltpu.VMEM((16, 8, 128), BF),
+            pltpu.VMEM((8, 128), BF),
+            pltpu.VMEM((2, 4, 8, 128), BF),
             pltpu.SemaphoreType.DMA((12,)),
             pltpu.SemaphoreType.DMA((N_STAGE,)),
             pltpu.SemaphoreType.DMA((N_STAGE,)),

time: 44.2 us -> 44.4 us (level)
  no operation moved by 1% of the time
where the time goes in v6:
time: 44.4 us; the launch traced here: 44.3 us
  Pallas kernels  44.3 us (100%)
    pallas_call x1, Pallas kernels, per_device(): pl.pallas_call(kernel, out_shape=(jax.ShapeDtypeStruct((R, 1024), BF), ja...  43.4 us
    pallas_call x1, Pallas kernels, per_device(): pl.pallas_call(lift, out_shape=jax.ShapeDtypeStruct((R, LEAF, 256), F32),...  0.94 us

profile of v6, /device:TPU:1, one launch (start us, length us, event | category | flops | bytes accessed | tf_op | source)
XLA Modules:
  0.0 44.3 jit_solution(1292100283678636983)
XLA Ops:
  0.0 0.0 copy-start
  0.0 43.4 %shard_map.118 = (bf16[16,1024]{1,0:T(8,128)(2,1)S(1)}, f32[16,16,256]{2,1,0:T(8,128)S(1)}) custom-call(bf16[16,16,256]{2,1,0:T(8,128)(2,1)} %src_h.1, bf16[1024,256]{1,0:T(8,128)(2,1)} %lf_h.1, bf16[4096,256]{1,0:T(8,128)(2,1)} %lp_h.1, bf16[640,1024]{1,0:T(8,128)(2,1)} %bu_h.1, bf16[1024,640]{1,0:T(8,128)(2,1)} %bd_h.1, bf16[256,768]{1,0:T(8,128)(2,1)} %u1_h.1, ...), custom_call_target="tpu_custom_call" | custom-call | tf_op jit(solution)/shard_map/pallas_call | solution.py:329
  43.4 0.0 copy-done
  43.4 0.9 %shard_map.119 = f32[16,16,256]{2,1,0:T(8,128)} custom-call(bf16[16,1024]{1,0:T(8,128)(2,1)S(1)} %get-tuple-element.7.lb_ref, f32[16,16,256]{2,1,0:T(8,128)S(1)} %get-tuple-element.8.part_ref, bf16[1024,256]{1,0:T(8,128)(2,1)S(1)} %copy-done), custom_call_target="tpu_custom_call" | custom-call | tf_op jit(solution)/shard_map/pallas_call | solution.py:372
Async XLA Ops:
  0.0 43.4 %copy-start = (bf16[1024,256]{1,0:T(8,128)(2,1)S(1)}, bf16[1024,256]{1,0:T(8,128)(2,1)}, u32[]{:S(2)}) copy-start(bf16[1024,256]{1,0:T(8,128)(2,1)} %ll_ref.1) | copy-start | bytes 1572868

commit v7 on v2

--- a/solution.py
+++ b/solution.py
@@ -11,8 +11,8 @@
 
 R = 16
 LEAF = 16
-ST_A, ST_AI, ST_B, ST_BI, ST_B2, ST_C1, ST_C2, ST_C3, ST_D, ST_E = range(10)
-N_STAGE = 10
+ST_A, ST_AI, ST_B, ST_BI, ST_B2, ST_C1, ST_C2, ST_C3, ST_D, ST_E, ST_B3 = range(11)
+N_STAGE = 11
 
 
 def nt(x, w):
@@ -29,7 +29,7 @@
     src, lf, lp, bu, bd, u1, d1, u2, d2, ur, dr,
     sp, pre_leaf, pre_mid, joint,
     a_s, a_r, ai_s, ai_r,
-    b_s, b_r, bi_s, bi_r, si, b2_r,
+    b_s, b_r, bi_s, bi_r, b2_s, b2_r, si,
     c1_s, c1_r, c2_s, c2_r, rs,
     d_all, e_all,
     load_sem, send_sem, recv_sem,
@@ -149,7 +149,9 @@
         send(b_s.at[to], b_r.at[dz * 4 + dy - 1], ST_B, in_plane(dz, dy))
     second_if = nn(second_piece, u2[:, :512])
     for j in range(4):
-        bi_s[2 * j], bi_s[2 * j + 1] = pack(second_if[:, 128 * j : 128 * j + 128])
+        bi_s[j] = second_if[:, 128 * j : 128 * j + 128].astype(BF)
+    for k in (2, 1, 3):
+        send(bi_s.at[(y + k) % 4], bi_r.at[k - 1], ST_BI, in_plane(0, k))
     l_bi.wait()
     box_if = nt(flux, bu[:384, :]).astype(BF)
     l_ur.wait()
@@ -172,9 +174,13 @@
             ST_C1,
             across(dx, dc, dy),
         )
-    for dz, dy in plane:
-        to = (zl + dz) % 2 * 4 + (y + dy) % 4
-        send(bi_s.at[to], bi_r.at[dz * 4 + dy - 1], ST_BI, in_plane(dz, dy))
+    arrived(bi_r, ST_BI)
+    block = bi_s[y].astype(F32)
+    for k in range(3):
+        block = block + bi_r[k].astype(F32)
+    b2_s[...] = block.astype(BF)
+    for dz in (2, 3, 1):
+        send(b2_s, b2_r.at[dz - 1], ST_B2, in_plane(dz, 0))
     l_lp.wait()
     for l in range(LEAF):
         part[l] = nn(sp[16 * l : 16 * l + 16, :], lp[256 * l : 256 * l + 256, :])
@@ -196,17 +202,12 @@
     c2_s[...] = mine.astype(BF)
     for dz in (4, 3, 5, 2, 6, 1, 7):
         send(c2_s, c2_r.at[dz - 1], ST_C2, along_z(dz))
-    arrived(bi_r, ST_BI)
-    own = zl % 2 * 4 + y
-    total = bi_s[own].astype(F32)
-    for k in range(15):
-        total = total + bi_r[k].astype(F32)
-    si[own] = total.astype(BF)
-    flip = zl + 1 - zl % 2 * 2
-    for dy in (2, 1, 3, 0):
-        send(si.at[own], si.at[own], ST_B2, (gx, (zh * 4 + flip) * 4 + (y + dy) % 4))
-    for dy in (2, 1, 3):
-        send(si.at[own], si.at[own], ST_B2, in_plane(0, dy))
+    arrived(b2_r, ST_B2)
+    for k in range(3):
+        block = block + b2_r[k].astype(F32)
+    si[y] = block.astype(BF)
+    for k in (2, 1, 3):
+        send(si.at[y], si.at[y], ST_B3, in_plane(0, k))
 
     arrived(c2_r, ST_C2)
     for k in range(7):
@@ -223,10 +224,8 @@
         joint[:, 256 * h : 256 * h + 256] = nn(
             bd[:, 384:], d1[:, 256 + 256 * h : 512 + 256 * h]
         ).astype(BF)
-    arrived(b2_r, ST_B2)
-    second_iface = jnp.concatenate(
-        [unpack(si[2 * j], si[2 * j + 1]) for j in range(4)], axis=1
-    )
+    arrived(bi_r, ST_B3)
+    second_iface = jnp.concatenate([si[j] for j in range(4)], axis=1)
     pre_mid[...] = nt(second_iface, d2[:, :512])
     arrived(c1_r, ST_C3)
     top = jnp.zeros((R, 64), F32)
@@ -252,6 +251,7 @@
     sent(b_r, ST_B)
     sent(bi_r, ST_BI)
     sent(b2_r, ST_B2)
+    sent(bi_r, ST_B3)
     sent(c1_r, ST_C1)
     sent(c2_r, ST_C2)
     sent(c1_r, ST_C3)
@@ -295,10 +295,11 @@
             pltpu.VMEM((3, 16, 256), BF),
             pltpu.VMEM((16, 8, 128), BF),
             pltpu.VMEM((15, 8, 128), BF),
-            pltpu.VMEM((8, 8, 128), BF),
-            pltpu.VMEM((15, 8, 128), BF),
-            pltpu.VMEM((8, 8, 128), BF),
-            pltpu.VMEM((7, 8, 128), BF),
+            pltpu.VMEM((4, 16, 128), BF),
+            pltpu.VMEM((3, 16, 128), BF),
+            pltpu.VMEM((16, 128), BF),
+            pltpu.VMEM((3, 16, 128), BF),
+            pltpu.VMEM((4, 16, 128), BF),
             pltpu.VMEM((2, 16, 8, 384), BF),
             pltpu.VMEM((31, 8, 384), BF),
             pltpu.VMEM((8, 384), BF),

time: 43.7 us -> 43.7 us (level)
  no operation moved by 1% of the time
where the time goes in v7:
time: 43.7 us; the launch traced here: 43.6 us
  Pallas kernels  43.6 us (100%)
    pallas_call x1, Pallas kernels, per_device(): pl.pallas_call(kernel, out_shape=(jax.ShapeDtypeStruct((R, 1024), BF), ja...  42.6 us
    pallas_call x1, Pallas kernels, per_device(): pl.pallas_call(lift, out_shape=jax.ShapeDtypeStruct((R, LEAF, 256), F32),...  0.94 us

profile of v7, /device:TPU:1, one launch (start us, length us, event | category | flops | bytes accessed | tf_op | source)
XLA Modules:
  0.0 43.6 jit_solution(15422209653152914497)
XLA Ops:
  0.0 0.0 copy-start
  0.0 42.6 %shard_map.118 = (bf16[16,1024]{1,0:T(8,128)(2,1)S(1)}, f32[16,16,256]{2,1,0:T(8,128)S(1)}) custom-call(bf16[16,16,256]{2,1,0:T(8,128)(2,1)} %src_h.1, bf16[1024,256]{1,0:T(8,128)(2,1)} %lf_h.1, bf16[4096,256]{1,0:T(8,128)(2,1)} %lp_h.1, bf16[640,1024]{1,0:T(8,128)(2,1)} %bu_h.1, bf16[1024,640]{1,0:T(8,128)(2,1)} %bd_h.1, bf16[256,768]{1,0:T(8,128)(2,1)} %u1_h.1, ...), custom_call_target="tpu_custom_call" | custom-call | tf_op jit(solution)/shard_map/pallas_call | solution.py:278
  42.7 0.0 copy-done
  42.7 0.9 %shard_map.119 = f32[16,16,256]{2,1,0:T(8,128)} custom-call(bf16[16,1024]{1,0:T(8,128)(2,1)S(1)} %get-tuple-element.7.lb_ref, f32[16,16,256]{2,1,0:T(8,128)S(1)} %get-tuple-element.8.part_ref, bf16[1024,256]{1,0:T(8,128)(2,1)S(1)} %copy-done), custom_call_target="tpu_custom_call" | custom-call | tf_op jit(solution)/shard_map/pallas_call | solution.py:318
Async XLA Ops:
  0.0 42.7 %copy-start = (bf16[1024,256]{1,0:T(8,128)(2,1)S(1)}, bf16[1024,256]{1,0:T(8,128)(2,1)}, u32[]{:S(2)}) copy-start(bf16[1024,256]{1,0:T(8,128)(2,1)} %ll_ref.1) | copy-start | bytes 1572868
